TPU v7x, 32 devices: a whole 2x2x4 slice. The times are simulated.
32 devices in a mesh: stn: 4 (over z), chan: 8 (over y, x, core).
Axes of the slice: x: 2, y: 2, z: 4, core: 2. Of those that a mesh axis runs over, the one named last changes fastest.
Arguments:
- voltages: bfloat16 [1024, 8, 8, 1024], P('stn', 'chan'), may hold values from -6 to 6
- fir_taps: float32 [8, 8, 1024], replicated, may hold values from -2.5 to 2.5
Outputs:
- visibilities: float32 [4, 64, 2, 1024, 1024], P(None, 'chan', None, 'stn')
All inputs are finite; a program needn't handle non-finite values.
Results may differ from a plain program's by a relative error of at most 0.0044.
Values may be sent and summed in bfloat16 or wider, within the bound.
No kernel may reach another device: no remote copies, remote signals or barrier semaphores. Data moves between devices by JAX's collectives and lax.ppermute only.
A program may use at most 192 MiB of HBM per device.

v0:
```python
import math

import jax
import jax.numpy as jnp
from jax import lax
from jax.sharding import PartitionSpec as P

AVG = 16


def shifted(block, axis, distance):
    devices = range(lax.axis_size(axis))
    route = [(i - distance, i) for i in devices if i - distance in devices]
    return lax.ppermute(block, axis, route)


def rotation(numbers, modulus):
    angles = (numbers % modulus).astype(jnp.float32) * jnp.float32(-2.0 * math.pi / modulus)
    return (jnp.cos(angles), jnp.sin(angles))


def split_pair(table):
    upper = table.astype(jnp.bfloat16)
    lower = (table - upper.astype(jnp.float32)).astype(jnp.bfloat16)
    return (upper, lower)


def complex_table(real_part, imag_part, axis_at):
    first = jnp.stack([real_part, imag_part], axis=-1)
    second = jnp.stack([-imag_part, real_part], axis=-1)
    return jnp.stack([first, second], axis=axis_at)


def per_device(voltages, fir_taps):
    inputs_dev, _, frames_dev, slot_count = voltages.shape
    phases = fir_taps.shape[0]
    tap_count = fir_taps.shape[1]
    lane_count = lax.axis_size("chan")
    groups = lane_count // phases
    position = lax.axis_index("chan")
    my_phase = position % phases
    my_group = position // phases
    recent = voltages[:, 0]
    if groups > 1:
        earlier = shifted(voltages[:, 0, frames_dev - (tap_count - 1) :, :], "chan", phases)
    else:
        earlier = jnp.zeros((inputs_dev, tap_count - 1, slot_count), voltages.dtype)
    series = jnp.concatenate([earlier, recent], axis=1)
    coeffs = lax.dynamic_index_in_dim(fir_taps, my_phase, 0, keepdims=False)
    frame_ids = my_group * frames_dev + jnp.arange(frames_dev, dtype=jnp.int32)
    keep_mask = (frame_ids >= tap_count - 1).astype(jnp.float32)
    filtered = sum(
        (
            coeffs[tap_index]
            * series[:, tap_count - 1 - tap_index : tap_count - 1 - tap_index + frames_dev].astype(
                jnp.float32
            )
            for tap_index in range(tap_count)
        )
    )
    filtered = filtered * keep_mask[None, :, None]
    better = lax.Precision.HIGH
    split_len = slot_count // phases
    folded = filtered.reshape(inputs_dev, frames_dev, split_len, phases)
    slot_ids = jnp.arange(split_len, dtype=jnp.int32)
    short_re, short_im = rotation(slot_ids[:, None] * slot_ids[None, :], split_len)
    short_table = jnp.stack([short_re, short_im], axis=-1)
    inner = jnp.einsum(
        "ifqr,qvc->rvcfi", folded, short_table, precision=better, preferred_element_type=jnp.float32
    )
    rest_ids = jnp.arange(phases, dtype=jnp.int32)
    freq_ids = jnp.arange(slot_count, dtype=jnp.int32).reshape(phases, split_len)
    twist_re, twist_im = rotation(
        (my_phase + phases * rest_ids)[:, None, None] * freq_ids[None], phases * slot_count
    )
    twist_table = complex_table(twist_re, twist_im, 3)
    branch = jnp.einsum(
        "rvcfi,ruvcd->uvfdi",
        inner,
        twist_table,
        precision=better,
        preferred_element_type=jnp.float32,
    )
    branch = branch.reshape(slot_count, 1, frames_dev, 2, inputs_dev).astype(jnp.bfloat16)
    band_count = phases // 2
    band_re, band_im = rotation(
        rest_ids[:, None] * jnp.arange(band_count, dtype=jnp.int32)[None, :], phases
    )
    band_table = complex_table(band_re, band_im, 1)
    band_upper, band_lower = split_pair(band_table)
    turned = lax.all_to_all(branch, "chan", split_axis=0, concat_axis=1, tiled=True)
    span_len = turned.shape[0]
    sources = turned.shape[1]
    item_count = turned.shape[2]
    grouped = turned.reshape(span_len, sources // phases, phases, item_count, 2, inputs_dev)
    phase_form = "wgpfci,pcbd->bwgfdi"
    total = jnp.einsum(
        phase_form, grouped, band_upper, preferred_element_type=jnp.float32
    ) + jnp.einsum(phase_form, grouped, band_lower, preferred_element_type=jnp.float32)
    spectra = total.astype(jnp.bfloat16)
    span_dev = spectra.shape[1]
    subs_dev = span_dev // AVG
    stacked = spectra.reshape(band_count, subs_dev, AVG * groups * frames_dev, 2, inputs_dev)
    columns = stacked.reshape(band_count, subs_dev, -1, inputs_dev)
    swapped = jnp.stack([stacked[:, :, :, 1], -stacked[:, :, :, 0]], axis=3).reshape(
        band_count, subs_dev, -1, inputs_dev
    )
    left_side = jnp.stack([columns, swapped], axis=2)
    spectra_count = groups * frames_dev - (tap_count - 1)
    scaling = 1.0 / (phases * slot_count * AVG * spectra_count)
    vis_form = "bsokn,bskw->bsonw"
    return (
        jnp.einsum(
            vis_form,
            left_side,
            lax.all_gather(columns, "stn", axis=3, tiled=True),
            preferred_element_type=jnp.float32,
        )
        * scaling
    )


def solution(mesh):
    return jax.shard_map(
        per_device,
        mesh=mesh,
        in_specs=(P("stn", "chan", None, None), P()),
        out_specs=P(None, "chan", None, "stn", None),
        check_vma=False,
    )
```

profile of v0, /device:TPU:0, one launch (start us, length us, event | category | flops | bytes accessed | tf_op | source)
XLA Modules:
  0.0 559.5 jit_solution(15071491346341078132)
XLA Ops:
  6.5 0.3 fusion.36
  6.9 0.2 fusion.38
  7.1 0.5 copy.40
  7.6 0.5 copy.41
  8.1 6.9 %copy.42 = bf16[256,1,8,1024]{0,3,2,1:T(8,128)(2,1)} copy(bf16[256,1,8,1024]{3,2,1,0:T(8,128)(2,1)} %param.2) | data formatting | bytes 8388608 | tf_op args[0]
  15.0 1.1 constant_dynamic-slice_fusion.6
  16.1 12.6 %multiply_bitcast_fusion = f32[256,8,128,8]{0,3,2,1:T(8,128)} fusion(bf16[256,8,1024]{0,2,1:T(8,128)(2,1)} %bitcast.96, f32[8]{0:T(128)S(1)} %compare_convert_fusion, f32[1024]{0:T(1024)S(1)} %bitcast.107, f32[1024]{0:T(1024)S(1)} %bitcast.101, f32[1024]{0:T(1024)S(1)} %bitcast.102, f32[1024]{0:T(1024)S(1)} %bitcast.103, f32[1024]{0:T(1024)S(1)} %bitcast.104, ...), kind=kLoop, calls=%fused_computation.24 | loop fusion | flops 50331648 | bytes 12615712 | tf_op jit(solution)/shard_map/reshape | solution.py:64
  28.7 9.1 %copy.44 = f32[256,8,128,8]{2,0,3,1:T(8,128)} copy(f32[256,8,128,8]{0,3,2,1:T(8,128)} %multiply_bitcast_fusion) | data formatting | bytes 16777216 | tf_op jit(solution)/shard_map/reshape | solution.py:64
  37.8 14.2 %fusion.18 = f32[8,128,2,8,256,1]{4,1,0,3,2,5:T(8,128)} fusion(f32[256,8,128,8]{2,0,3,1:T(8,128)} %copy.44, f32[128,128,1]{1,0,2:T(8,128)S(1)} %get-tuple-element.24, f32[128,128,1]{1,0,2:T(8,128)S(1)} %get-tuple-element.25), kind=kOutput, calls=%fused_computation.27 | convolution fusion | flops 3221258240 | bytes 25296896 | tf_op jit(solution)/shard_map/ifqr,qvc->rvcfi/dot_general | solution.py:68
  52.0 25.0 %fusion.3 = bf16[8,128,8,2,256]{4,0,2,3,1:T(8,128)(2,1)} fusion(f32[8,128,2,8,256,1]{4,1,0,3,2,5:T(8,128)} %fusion.18, f32[8,8,128,1,2]{0,1,3,4,2:T(8,128)S(1)} %bitcast.99, f32[8,8,128,1,2]{0,1,3,4,2:T(8,128)S(1)} %bitcast.98), kind=kOutput, calls=%fused_computation.12 | convolution fusion | flops 406880256 | bytes 25296896 | tf_op jit(solution)/shard_map/rvcfi,ruvcd->uvfdi/dot_general | solution.py:77
  77.0 8.5 %copy.46 = bf16[8,128,8,2,256]{4,2,3,1,0:T(8,128)(2,1)} copy(bf16[8,128,8,2,256]{4,0,2,3,1:T(8,128)(2,1)} %fusion.3) | data formatting | bytes 16777216 | tf_op jit(solution)/shard_map/convert_element_type | solution.py:84
  85.5 16.0 %all-to-all-start = ((bf16[1024,1,8,2,256]{4,2,3,1,0:T(8,128)(2,1)}), bf16[1024,1,8,2,256]{4,2,3,1,0:T(8,128)(2,1)}, u32[]{:S(2)}, u32[]{:S(2)}) async-start(bf16[1024,1,8,2,256]{4,2,3,1,0:T(8,128)(2,1)} %bitcast.95), calls=%async_computation | async-start | bytes 16777216 | tf_op jit(solution)/shard_map/all_to_all | solution.py:91
  101.5 0.0 all-gather.2.cloned.1.call-start
  101.6 0.1 fusion.52
  101.6 0.1 fusion.50
  101.7 94.6 %all-to-all-done = bf16[1024,1,8,2,256]{4,2,3,1,0:T(8,128)(2,1)} async-done(((bf16[1024,1,8,2,256]{4,2,3,1,0:T(8,128)(2,1)}), bf16[1024,1,8,2,256]{4,2,3,1,0:T(8,128)(2,1)}, u32[]{:S(2)}, u32[]{:S(2)}) %all-to-all-start) | async-done | bytes 8388640 | tf_op jit(solution)/shard_map/all_to_all | solution.py:91
  196.3 12.6 %fusion.8 = f32[4,2,128,8,256,1]{4,0,5,3,2,1:T(4,128)} fusion(bf16[8,128,1,8,2,256]{5,3,4,2,1,0:T(8,128)(2,1)} %bitcast.28, f32[8,1,4,2]{0,2,1,3:T(4,128)S(1)} %get-tuple-element.21, f32[8,1,4,2]{0,2,1,3:T(4,128)S(1)} %get-tuple-element.20), kind=kOutput, calls=%fused_computation.18 | convolution fusion | flops 67109504 | bytes 16777728 | tf_op jit(solution)/shard_map/wgpfci,pcbd->bwgfdi/dot_general | solution.py:99
  208.9 16.7 %fusion.7 = bf16[4,2,128,8,256]{4,0,3,2,1:T(4,128)(2,1)} fusion(f32[4,2,128,8,256,1]{4,0,5,3,2,1:T(4,128)} %fusion.8, bf16[8,128,1,8,2,256]{5,3,4,2,1,0:T(8,128)(2,1)} %bitcast.28, f32[8,1,4,2]{0,2,1,3:T(4,128)S(1)} %get-tuple-element.21, f32[8,1,4,2]{0,2,1,3:T(4,128)S(1)} %get-tuple-element.20), kind=kOutput, calls=%fused_computation.17 | convolution fusion | flops 71303680 | bytes 20972032 | tf_op jit(solution)/shard_map/wgpfci,pcbd->bwgfdi/dot_general | solution.py:97
  225.6 4.3 copy.48
  229.9 0.0 copy-start
  229.9 1.9 copy-done
  231.8 2.8 copy.54
  234.6 0.0 all-gather.2.cloned.1.call-update
  234.6 7.5 %copy.51 = bf16[4,8,1,256,256]{3,4,2,1,0:T(8,128)(2,1)} copy(bf16[4,8,1,256,256]{4,0,3,1,2:T(4,128)(2,1)} %bitcast.94) | data formatting | bytes 8388608 | tf_op jit(solution)/shard_map/stack;reshape;reshape | solution.py:108
  242.1 3.8 fusion.58
  245.9 1.2 copy.68
  247.1 2.4 copy_negate_fusion
  249.5 2.3 pad_maximum_fusion
  251.8 7.6 %copy.52 = bf16[4,8,1,256,256]{3,4,2,1,0:T(8,128)(2,1)} copy(bf16[4,8,1,256,256]{4,1,3,0,2:T(8,128)(2,1)} %bitcast.97) | data formatting | bytes 8388608 | tf_op jit(solution)/shard_map/stack;reshape | solution.py:108
  259.4 261.7 %all-gather.2.cloned.1.call-done = bf16[4,8,256,1024]{3,2,1,0:T(8,128)(2,1)} async-done(((bf16[4,8,256,256]{3,2,1,0:T(8,128)(2,1)}), bf16[4,8,256,1024]{3,2,1,0:T(8,128)(2,1)}) %all-gather.2.cloned.1.call-update) | async-done | bytes 16777232 | tf_op jit(solution)/shard_map/all_gather | solution.py:116
  521.2 31.3 %convolution_multiply_fusion = f32[4,8,2,256,1024]{4,3,2,1,0:T(8,128)} fusion(bf16[4,8,256,1024]{3,2,1,0:T(8,128)(2,1)} %all-gather.2.cloned.1.call-done, bf16[4,8,1,256,256]{3,4,2,1,0:T(8,128)(2,1)} %copy.52, bf16[4,8,1,256,256]{3,4,2,1,0:T(8,128)(2,1)} %copy.51), kind=kOutput, calls=%fused_computation | convolution fusion | flops 8610906112 | bytes 92274688 | tf_op jit(solution)/shard_map/bsokn,bskw->bsonw/dot_general | solution.py:113
  (5 shorter events, 0.0 us)
Async XLA Ops:
  85.5 110.8 %all-to-all-start = ((bf16[1024,1,8,2,256]{4,2,3,1,0:T(8,128)(2,1)}), bf16[1024,1,8,2,256]{4,2,3,1,0:T(8,128)(2,1)}, u32[]{:S(2)}, u32[]{:S(2)}) async-start(bf16[1024,1,8,2,256]{4,2,3,1,0:T(8,128)(2,1)} %bitcast.95), calls=%async_computation | async-start | bytes 16777216 | tf_op jit(solution)/shard_map/all_to_all | solution.py:91
  101.5 419.6 %all-gather.2.cloned.1.call-start = ((), (), s32[]{:S(2)}) async-start(), calls=%async_computation.1 | async-start | bytes 20971520 | tf_op jit(solution)/shard_map/all_gather | solution.py:116
  229.9 2.0 copy-start
Sparse Core Ops, SparseCore 0:
  234.8 286.3 all-gather.1
where the time goes:
time: 566 us; the launch traced here: 560 us
  waiting for transfers between devices  356 us (63%)
  matrix products  99.8 us (18%)
  local copies, waits for them, and re-layouts  55.6 us (10%)
  other arithmetic  18 us (3%)
  starting transfers between devices  16 us (3%)
  between operations  13.7 us (2%)
    all_gather x1, waiting for transfers between devices, per_device(): lax.all_gather(columns, 'stn', axis=3, tiled=True)  262 us
    all_to_all x1, waiting for transfers between devices, per_device(): lax.all_to_all(branch, 'chan', split_axis=0, concat_axis=1, tiled=True)  94.6 us
    dot_general x1, matrix products, per_device(): jnp.einsum(vis_form, left_side, lax.all_gather(columns, 'stn', axis=3, ti...  31.3 us
    dot_general x1, matrix products, per_device(): jnp.einsum('rvcfi,ruvcd->uvfdi', inner, twist_table, precision=better, pr...  25 us
    dot_general x1, matrix products, per_device(): jnp.einsum(phase_form, grouped, band_upper, preferred_element_type=jnp.fl...  16.7 us
    all_to_all x1, starting transfers between devices, per_device(): lax.all_to_all(branch, 'chan', split_axis=0, concat_axis=1, tiled=True)  16 us
    another operation x2, local copies, waits for them, and re-layouts, per_device(): left_side = jnp.stack([columns, swapped], axis=2)  15 us
    dot_general x1, matrix products, per_device(): jnp.einsum('ifqr,qvc->rvcfi', folded, short_table, precision=better, pref...  14.2 us
  transfers between devices with their start and end apart: 2, of which 2 were waited for; matrix products, arithmetic and copies ran while one was open for 4% of the time, Pallas kernels for 0%

commit v1 on v0

--- a/solution.py
+++ b/solution.py
@@ -1,11 +1,18 @@
+import functools
 import math
 
 import jax
 import jax.numpy as jnp
+import numpy as np
 from jax import lax
+from jax.experimental import pallas as pl
+from jax.experimental.pallas import tpu as pltpu
 from jax.sharding import PartitionSpec as P
 
 AVG = 16
+LANES = 128
+PER_PART = 2
+SLOTS_OUT = 8
 
 
 def shifted(block, axis, distance):
@@ -31,7 +38,7 @@
     return jnp.stack([first, second], axis=axis_at)
 
 
-def per_device(voltages, fir_taps):
+def all_frames(voltages, fir_taps):
     inputs_dev, _, frames_dev, slot_count = voltages.shape
     phases = fir_taps.shape[0]
     tap_count = fir_taps.shape[1]
@@ -120,6 +127,350 @@
     )
 
 
+def split_value(value):
+    upper = value.astype(jnp.bfloat16)
+    lower = (value - upper.astype(jnp.float32)).astype(jnp.bfloat16)
+    return upper, lower
+
+
+def weighted(terms, weights):
+    total = None
+    for term, weight in zip(terms, weights):
+        if abs(weight) < 1e-9:
+            continue
+        part = term if abs(abs(weight) - 1.0) < 1e-9 else term * jnp.float32(abs(weight))
+        if total is None:
+            total = -part if weight < 0 else part
+        else:
+            total = total - part if weight < 0 else total + part
+    return total
+
+
+def turn_weights(count, step, radix):
+    angles = [-2.0 * math.pi * ((k * step) % radix) / radix for k in range(count)]
+    return [math.cos(a) for a in angles], [math.sin(a) for a in angles]
+
+
+def half_sums(pieces):
+    half = len(pieces) // 2
+    sums = [pieces[k] + pieces[k + half] for k in range(half)]
+    differences = [pieces[k] - pieces[k + half] for k in range(half)]
+    return sums, differences
+
+
+def branch_tables(phases, radix, dests):
+    slots = radix * LANES
+    near = LANES // dests
+    v = np.repeat(np.arange(LANES).reshape(dests, 1, near), 2, axis=1).reshape(-1, 1)
+    is_imag = np.broadcast_to(np.arange(2)[None, :, None], (dests, 2, near)).reshape(-1, 1)
+    column = np.arange(2 * LANES)[None, :]
+    b, half = column % LANES, column // LANES
+    angle = -2.0 * np.pi * ((v * b) % LANES) / LANES + 0.5 * np.pi * (half - is_imag)
+    far = np.stack([np.cos(angle), np.sin(angle)])
+    phase = np.arange(phases)
+    angle = -2.0 * np.pi * ((v * phase[None, :]) % slots) / slots
+    row = np.stack([np.cos(angle), np.sin(angle)], axis=1).transpose(2, 0, 1)
+    row = np.broadcast_to(row[..., None], row.shape + (1,))
+    u = np.arange(radix)[None, :, None]
+    turns = (u * (phase[:, None, None] + phases * b[None])) % (phases * slots)
+    angle = -2.0 * np.pi * turns / (phases * slots)
+    low = np.stack([np.cos(angle), np.sin(angle)], axis=1)
+    mirrored = (u > radix // 2) & (half[None] == 1)
+    low = np.where(mirrored[:, None], -low, low)
+    return far.astype(np.float32), row[..., 0].astype(np.float32), low.astype(np.float32)
+
+
+def branch_kernel(radix, dests, place_ref, volt_ref, taps_ref, far_ref, row_ref, low_ref, *rest):
+    outs, (volts, y, table, block, volt_sems, out_sems) = rest[:-6], rest[-6:]
+    me = place_ref[0]
+    parts, rows = volts.shape[0], volts.shape[1]
+    loads = [
+        pltpu.make_async_copy(volt_ref.at[pl.ds(i * rows, rows), 0], volts.at[i], volt_sems.at[i])
+        for i in range(parts)
+    ]
+    for load in loads:
+        load.start()
+    row_cos, row_sin = row_ref[0, :, 0:1], row_ref[0, :, 1:2]
+    far_cos = far_ref[0] * row_cos - far_ref[1] * row_sin
+    far_sin = far_ref[0] * row_sin + far_ref[1] * row_cos
+    for u in range(radix):
+        entry = far_cos * low_ref[0, 0, u : u + 1] - far_sin * low_ref[0, 1, u : u + 1]
+        table[0, u], table[1, u] = split_value(entry)
+    taps = taps_ref[0]
+    by_frame = jnp.concatenate([taps[k : k + 1] for k in reversed(range(taps.shape[0]))], axis=0)
+    together = LANES // rows
+    for i in range(0, parts, together):
+        filtered = []
+        for k in range(i, i + together):
+            loads[k].wait()
+            filtered.append(jnp.sum(volts[k].astype(jnp.float32) * by_frame[None], axis=1))
+        filtered = jnp.concatenate(filtered, axis=0)
+        pieces = [filtered[:, a * LANES : (a + 1) * LANES].T for a in range(radix)]
+        sums, differences = half_sums(pieces)
+        for u in range(radix // 2 + 1):
+            terms = differences if u % 2 else sums
+            for part, weights in enumerate(turn_weights(radix // 2, u, radix)):
+                value = weighted(terms, weights)
+                if value is None:
+                    value = jnp.zeros_like(pieces[0])
+                at = (pl.ds(part * LANES, LANES), pl.ds(i * rows, LANES))
+                y[(u, 0) + at], y[(u, 1) + at] = split_value(value)
+    inputs = y.shape[3]
+    for u in range(radix):
+        source = min(u, radix - u)
+        total = jnp.dot(table[0, u], y[source, 0], preferred_element_type=jnp.float32)
+        total += jnp.dot(table[0, u], y[source, 1], preferred_element_type=jnp.float32)
+        total += jnp.dot(table[1, u], y[source, 0], preferred_element_type=jnp.float32)
+        block[:, u] = total.astype(jnp.bfloat16).reshape(dests, -1, inputs)
+    stores = []
+    for k in range(dests):
+        dest = lax.bitwise_xor(me, k)
+        stores.append(pltpu.make_async_copy(block.at[dest], outs[k], out_sems.at[k]))
+        stores[-1].start()
+    for store in stores:
+        store.wait()
+
+
+def branch_of(voltages, fir_taps, me, dests):
+    inputs, _, frames, slots = voltages.shape
+    phases, tap_count, _ = fir_taps.shape
+    radix = slots // LANES
+    rows = LANES // dests
+    far, row, low = branch_tables(phases, radix, dests)
+    parts = 8
+    block = inputs // parts
+    place = lambda *shape: pl.BlockSpec((1,) + shape, lambda i, ph: (ph[0],) + (0,) * len(shape))
+    outs = dests
+    return pl.pallas_call(
+        functools.partial(branch_kernel, radix, dests),
+        out_shape=[jax.ShapeDtypeStruct((radix, 2 * rows, inputs), jnp.bfloat16)] * outs,
+        grid_spec=pltpu.PrefetchScalarGridSpec(
+            num_scalar_prefetch=1,
+            grid=(1,),
+            in_specs=[
+                pl.BlockSpec(memory_space=pl.ANY),
+                place(tap_count, slots),
+                pl.BlockSpec(far.shape, lambda i, ph: (0, 0, 0)),
+                place(*row.shape[1:]),
+                place(*low.shape[1:]),
+            ],
+            out_specs=[pl.BlockSpec(memory_space=pl.ANY)] * outs,
+            scratch_shapes=[
+                pltpu.VMEM((parts, block, frames, slots), jnp.bfloat16),
+                pltpu.VMEM((radix // 2 + 1, 2, 2 * LANES, inputs), jnp.bfloat16),
+                pltpu.VMEM((2, radix, 2 * LANES, 2 * LANES), jnp.bfloat16),
+                pltpu.VMEM((dests, radix, 2 * rows, inputs), jnp.bfloat16),
+                pltpu.SemaphoreType.DMA((parts,)),
+                pltpu.SemaphoreType.DMA((outs,)),
+            ],
+        ),
+        cost_estimate=pl.CostEstimate(
+            flops=6 * radix * inputs * (2 * LANES) ** 2,
+            transcendentals=0,
+            bytes_accessed=2 * voltages.size + 4 * inputs * slots,
+        ),
+        name="branch",
+    )(me.reshape(1), voltages, fir_taps, far, row, low)
+
+
+def band_kernel(place_ref, *rest):
+    turned, sems = rest[-2:]
+    phases, radix, rows, _ = turned.shape
+    blocks, outs = rest[:phases], rest[phases:-2]
+    me = place_ref[0]
+    loads = [
+        pltpu.make_async_copy(blocks[k], turned.at[lax.bitwise_xor(me, k)], sems.at[k]) for k in range(phases)
+    ]
+    for load in loads:
+        load.start()
+    for load in loads:
+        load.wait()
+    near = rows // 2
+    for u in range(radix):
+        pair = [turned[p, u].astype(jnp.float32) for p in range(phases)]
+        re, im = [x[:near] for x in pair], [x[near:] for x in pair]
+        re_pair, im_pair = half_sums(re), half_sums(im)
+        at = u * rows
+        for c in range(phases // 2):
+            cos_w, sin_w = turn_weights(phases // 2, c, phases)
+            terms = re_pair[c % 2] + im_pair[c % 2]
+            out_ref, band = outs[c // PER_PART], c % PER_PART
+            out_ref[band, at : at + near] = weighted(terms, cos_w + [-w for w in sin_w]).astype(jnp.bfloat16)
+            out_ref[band, at + near : at + rows] = weighted(terms, sin_w + cos_w).astype(jnp.bfloat16)
+
+
+def bands_of(blocks, me):
+    phases = len(blocks)
+    radix, rows, inputs = blocks[0].shape
+    bands, depth = phases // 2, radix * rows
+    return pl.pallas_call(
+        band_kernel,
+        out_shape=[jax.ShapeDtypeStruct((PER_PART, depth, inputs), jnp.bfloat16)] * (bands // PER_PART),
+        in_specs=[pl.BlockSpec(memory_space=pltpu.SMEM)] + [pl.BlockSpec(memory_space=pl.ANY)] * phases,
+        out_specs=[pl.BlockSpec(memory_space=pltpu.VMEM)] * (bands // PER_PART),
+        scratch_shapes=[
+            pltpu.VMEM((phases, radix, rows, inputs), jnp.bfloat16),
+            pltpu.SemaphoreType.DMA((phases,)),
+        ],
+        cost_estimate=pl.CostEstimate(flops=0, transcendentals=0, bytes_accessed=6 * bands * depth * inputs),
+        name="bands",
+    )(me.reshape(1), *blocks)
+
+
+def left_kernel(near, *refs):
+    rights, left_ref = refs[:-1], refs[-1]
+    for c in range(left_ref.shape[1]):
+        right = rights[c // PER_PART][c % PER_PART]
+        turned = right.astype(jnp.float32).T
+        left_ref[0, c] = turned.astype(jnp.bfloat16)
+        depth = turned.shape[1]
+        real = lax.broadcasted_iota(jnp.int32, turned.shape, 1) % (2 * near) < near
+        ahead = pltpu.roll(turned, depth - near, 1)
+        behind = pltpu.roll(turned, near, 1)
+        left_ref[1, c] = jnp.where(real, ahead, -behind).astype(jnp.bfloat16)
+
+
+def left_of(rights, near):
+    _, depth, inputs = rights[0].shape
+    bands = PER_PART * len(rights)
+    return pl.pallas_call(
+        functools.partial(left_kernel, near),
+        out_shape=jax.ShapeDtypeStruct((2, bands, inputs, depth), jnp.bfloat16),
+        in_specs=[pl.BlockSpec(memory_space=pltpu.VMEM)] * len(rights),
+        out_specs=pl.BlockSpec(memory_space=pltpu.VMEM),
+        cost_estimate=pl.CostEstimate(flops=0, transcendentals=0, bytes_accessed=6 * bands * depth * inputs),
+        name="left",
+    )(*rights)
+
+
+def correlate_kernel(near, group, parts, either, scaling, place_ref, left_ref, *rest):
+    out_ref, buffer, sems = rest[-3:]
+    rights = rest[: len(parts) * either]
+    slots, _, _, width = buffer.shape
+    depth = left_ref.shape[3]
+    subs = near // group
+    lanes = lax.broadcasted_iota(jnp.int32, (16, depth), 1) % near // group
+    columns = pl.ds(pl.multiple_of(place_ref[0] * width, width), width)
+
+    def store(c, k, slot):
+        return pltpu.make_async_copy(buffer.at[slot], out_ref.at[c, k, :, :, columns], sems.at[slot])
+
+    pending = [None] * slots
+    for at, part in enumerate(parts):
+        for band in range(PER_PART):
+            c = part * PER_PART + band
+            right = rights[at * either][band]
+            if either > 1:
+                right = jnp.where(place_ref[1] > 0, right, rights[at * either + 1][band])
+            for k in range(subs):
+                slot = ((at * PER_PART + band) * subs + k) % slots
+                if pending[slot] is not None:
+                    pending[slot].wait()
+                mask = (lanes == k).astype(jnp.float32).astype(jnp.bfloat16)[:1]
+                for half in range(2):
+                    product = jnp.dot(left_ref[half, c] * mask, right, preferred_element_type=jnp.float32)
+                    buffer[slot, half] = product * scaling
+                pending[slot] = store(c, k, slot)
+                pending[slot].start()
+    for copy in pending:
+        copy.wait()
+
+
+def correlate(left, parts, rights, place, total, near, radix, scaling, shape):
+    _, _, inputs, depth = left.shape
+    group = AVG // radix
+    subs = near // group
+    fresh = total is None
+    either = len(rights[0])
+    flat = [right for pair in rights for right in pair]
+    done = len(parts) * PER_PART
+    return pl.pallas_call(
+        functools.partial(correlate_kernel, near, group, tuple(parts), either, scaling),
+        out_shape=jax.ShapeDtypeStruct(shape, jnp.float32),
+        in_specs=[pl.BlockSpec(memory_space=pltpu.SMEM)]
+        + [pl.BlockSpec(memory_space=pltpu.VMEM)] * (1 + len(flat))
+        + ([] if fresh else [pl.BlockSpec(memory_space=pl.ANY)]),
+        out_specs=pl.BlockSpec(memory_space=pl.ANY),
+        scratch_shapes=[
+            pltpu.VMEM((SLOTS_OUT, 2, inputs, inputs), jnp.float32),
+            pltpu.SemaphoreType.DMA((SLOTS_OUT,)),
+        ],
+        input_output_aliases={} if fresh else {2 + len(flat): 0},
+        cost_estimate=pl.CostEstimate(
+            flops=4 * done * subs * inputs * inputs * depth,
+            transcendentals=0,
+            bytes_accessed=8 * done * subs * inputs * inputs,
+        ),
+        name="correlate",
+    )(*([place, left] + flat + ([] if fresh else [total])))
+
+
+def near_memory(array):
+    return pltpu.with_memory_space_constraint(array, pltpu.VMEM)
+
+
+def far_memory(array):
+    return pltpu.with_memory_space_constraint(array, pltpu.HBM)
+
+
+def one_frame(voltages, fir_taps):
+    inputs, _, _, slots = voltages.shape
+    phases = fir_taps.shape[0]
+    dests = lax.axis_size("chan")
+    radix = slots // LANES
+    near = LANES // dests
+    place = lax.axis_index("chan")
+    branch = branch_of(voltages, fir_taps, place, dests)
+    turned = [branch[0]] + [None] * (dests - 1)
+    for k in reversed(range(1, dests)):
+        turned[k] = far_memory(lax.ppermute(branch[k], "chan", [(i, i ^ k) for i in range(dests)]))
+    own = bands_of(turned, place)
+    parts = list(range(len(own)))
+    stations = lax.axis_size("stn")
+    me = lax.axis_index("stn")
+    shape = (phases // 2, near * radix // AVG, 2, inputs, inputs * stations)
+    scaling = 1.0 / (phases * slots * AVG)
+    inner = (me == 1) | (me == 2)
+    add = functools.partial(correlate, near=near, radix=radix, scaling=scaling, shape=shape)
+
+    def spot(k):
+        return jnp.stack([me ^ k, inner.astype(jnp.int32)])
+
+    two = [near_memory(lax.ppermute(x, "stn", [(i, i ^ 2) for i in range(4)])) for x in own]
+    one = [near_memory(lax.ppermute(x, "stn", [(i, i ^ 1) for i in range(4)])) for x in own]
+    middle = [near_memory(lax.ppermute(x, "stn", [(1, 2), (2, 1)])) for x in own]
+    relay = [near_memory(lax.ppermute(x, "stn", [(1, 0), (2, 3)])) for x in two]
+    left = left_of(own, near)
+    total = add(left, parts, [[x] for x in own], spot(0), None)
+    for h in parts:
+        total = add(left, [h], [[two[h]]], spot(2), total)
+    total = add(left, parts, [[x] for x in one], spot(1), total)
+    for h in parts:
+        total = add(left, [h], [[middle[h], relay[h]]], spot(3), total)
+    return total
+
+
+def per_device(voltages, fir_taps):
+    inputs, _, frames, slots = voltages.shape
+    phases, tap_count, _ = fir_taps.shape
+    lanes = lax.axis_size("chan")
+    radix = slots // LANES
+    fits = (
+        lanes == phases
+        and frames == tap_count
+        and phases & (phases - 1) == 0
+        and phases % 2 == 0
+        and slots % LANES == 0
+        and radix % 2 == 0
+        and AVG % radix == 0
+        and LANES % (16 * lanes) == 0
+        and phases // 2 % PER_PART == 0
+        and lax.axis_size("stn") == 4
+        and inputs % LANES == 0
+    )
+    return one_frame(voltages, fir_taps) if fits else all_frames(voltages, fir_taps)
+
+
 def solution(mesh):
     return jax.shard_map(
         per_device,

time: 566 us -> 83.1 us (0.15); the launches traced: 560 us -> 82.4 us
  waiting for transfers between devices: 356 us -> 10.3 us
  matrix products: 99.8 us -> 0 us
  local copies, waits for them, and re-layouts: 55.6 us -> 0.7 us
  Pallas kernels: 0 us -> 50.2 us
  other arithmetic: 18 us -> 2.55 us
  between operations: 13.7 us -> 0.37 us
    all_gather x1 -> x0, waiting for transfers between devices: 262 us -> none  [per_device(): lax.all_gather(columns, 'stn', axis=3, tiled=True)]
    dot_general x5 -> x0, matrix products: 99.8 us -> none  [the longest x1 31.3 us: per_device(): jnp.einsum(vis_form, left_side, lax.all_gather(columns, 'stn', axis=3, ti...]
    all_to_all x1 -> x0, waiting for transfers between devices: 94.6 us -> none  [per_device(): lax.all_to_all(branch, 'chan', split_axis=0, concat_axis=1, tiled=True)]
    pallas_call x0 -> x9, Pallas kernels: none -> 50.2 us  [the longest x6 37.6 us: correlate(): pl.pallas_call(functools.partial(correlate_kernel, near, group, tuple(par...]
    another operation x5 -> x0, local copies, waits for them, and re-layouts: 18.8 us -> none  [the longest x2 15 us: per_device(): left_side = jnp.stack([columns, swapped], axis=2)]
    ppermute x0 -> x15, starting transfers between devices: none -> 18.3 us  [the longest x7 8.67 us: one_frame(): lax.ppermute(branch[k], 'chan', [(i, i ^ k) for i in range(dests)])]
    all_to_all x1 -> x0, starting transfers between devices: 16 us -> none  [per_device(): lax.all_to_all(branch, 'chan', split_axis=0, concat_axis=1, tiled=True)]
    convert_element_type x2 -> x0, local copies, waits for them, and re-layouts: 12.8 us -> none  [the longest x1 8.52 us: per_device(): branch.reshape(slot_count, 1, frames_dev, 2, inputs_dev)]
  transfers between devices with their start and end apart: 2 -> 15, of which waited for: 2 -> 2; matrix products, arithmetic and copies ran while one was open for 4% -> 3% of each run, Pallas kernels for 0% -> 43%
where the time goes in v1:
time: 83.1 us; the launch traced here: 82.4 us
  Pallas kernels  50.2 us (60%)
  starting transfers between devices  18.3 us (22%)
  waiting for transfers between devices  10.3 us (12%)
  other arithmetic  2.55 us (3%)
    pallas_call x6, Pallas kernels, correlate(): pl.pallas_call(functools.partial(correlate_kernel, near, group, tuple(par...  37.6 us
    ppermute x7, starting transfers between devices, one_frame(): lax.ppermute(branch[k], 'chan', [(i, i ^ k) for i in range(dests)])  8.67 us
    pallas_call x1, Pallas kernels, branch_of(): pl.pallas_call(functools.partial(branch_kernel, radix, dests), out_shape=...  7.47 us
    ppermute x7, waiting for transfers between devices, one_frame(): lax.ppermute(branch[k], 'chan', [(i, i ^ k) for i in range(dests)])  6.35 us
    ppermute x2, waiting for transfers between devices, one_frame(): lax.ppermute(x, 'stn', [(i, i ^ 2) for i in range(4)])  3.92 us
    ppermute x2, starting transfers between devices, one_frame(): lax.ppermute(x, 'stn', [(i, i ^ 2) for i in range(4)])  2.99 us
    pallas_call x1, Pallas kernels, left_of(): pl.pallas_call(functools.partial(left_kernel, near), out_shape=jax.ShapeD...  2.58 us
    ppermute x2, starting transfers between devices, one_frame(): relay = [near_memory(lax.ppermute(x, 'stn', [(1, 0), (2, 3)])) for x in two]  2.58 us
  transfers between devices with their start and end apart: 15, of which 2 were waited for; matrix products, arithmetic and copies ran while one was open for 3% of the time, Pallas kernels for 43%

profile of v1, /device:TPU:0, one launch (start us, length us, event | category | flops | bytes accessed | tf_op | source)
XLA Modules:
  0.0 82.4 jit_solution(6694050832348713183)
XLA Ops:
  0.0 7.5 %branch.1 = (bf16[8,32,256]{2,1,0:T(8,128)(2,1)}, bf16[8,32,256]{2,1,0:T(8,128)(2,1)}, bf16[8,32,256]{2,1,0:T(8,128)(2,1)}, bf16[8,32,256]{2,1,0:T(8,128)(2,1)},...) custom-call(s32[1]{0:T(128)} %bitcast.2.place_ref, ...), custom_call_target="tpu_custom_call" | custom-call | flops 805306368 | bytes 5242880 | tf_op jit(solution)/shard_map/branch/pallas_call | solution.py:244
  7.5 0.5 collective-permute-start
  8.0 2.6 %collective-permute-start.1 = (bf16[8,32,256]{2,1,0:T(8,128)(2,1)}, bf16[8,32,256]{2,1,0:T(8,128)(2,1)S(1)}, u32[]{:S(2)}, u32[]{:S(2)}) collective-permute-start(bf16[8,32,256]{2,1,0:T(8,128)(2,1)} %get-tuple-element.17), channel_id=1, source_target_pairs={{0,2},{1,3},{2,0},{3,1},{4,6},{5,7},{6,4},{7,5},{8,10},{9,11},{10,... | collective-permute-start | bytes 393224 | tf_op jit(solution)/shard_map/ppermute | solution.py:426
  10.6 0.0 collective-permute-start.2
  10.6 1.8 %collective-permute-start.3 = (bf16[8,32,256]{2,1,0:T(8,128)(2,1)}, bf16[8,32,256]{2,1,0:T(8,128)(2,1)S(1)}, u32[]{:S(2)}, u32[]{:S(2)}) collective-permute-start(bf16[8,32,256]{2,1,0:T(8,128)(2,1)} %get-tuple-element.19), channel_id=1, source_target_pairs={{0,4},{1,5},{2,6},{3,7},{4,0},{5,1},{6,2},{7,3},{8,12},{9,13},{10,... | collective-permute-start | bytes 393224 | tf_op jit(solution)/shard_map/ppermute | solution.py:426
  12.4 0.0 collective-permute-start.4
  12.4 0.6 pad_add_fusion.3.place_ref
  13.0 0.0 collective-permute-done.rest_1_
  13.0 0.0 copy-start
  13.0 2.6 %collective-permute-start.5 = (bf16[8,32,256]{2,1,0:T(8,128)(2,1)}, bf16[8,32,256]{2,1,0:T(8,128)(2,1)S(1)}, u32[]{:S(2)}, u32[]{:S(2)}) collective-permute-start(bf16[8,32,256]{2,1,0:T(8,128)(2,1)} %get-tuple-element.21), channel_id=1, source_target_pairs={{0,6},{1,7},{2,4},{3,5},{4,2},{5,3},{6,0},{7,1},{8,14},{9,15},{10,... | collective-permute-start | bytes 393224 | tf_op jit(solution)/shard_map/ppermute | solution.py:426
  15.7 0.0 collective-permute-done.1.rest_2_
  15.7 0.0 copy-start.1
  15.7 1.1 %collective-permute-start.6 = (bf16[8,32,256]{2,1,0:T(8,128)(2,1)}, bf16[8,32,256]{2,1,0:T(8,128)(2,1)S(1)}, u32[]{:S(2)}, u32[]{:S(2)}) collective-permute-start(bf16[8,32,256]{2,1,0:T(8,128)(2,1)} %get-tuple-element.22), channel_id=1, source_target_pairs={{0,7},{1,6},{2,5},{3,4},{4,3},{5,2},{6,1},{7,0},{8,15},{9,14},{10,... | collective-permute-start | bytes 393224 | tf_op jit(solution)/shard_map/ppermute | solution.py:426
  16.8 0.7 pad_add_fusion.2.place_ref
  17.4 0.7 pad_add_fusion.1.place_ref
  18.1 0.0 collective-permute-done.2.rest_3_
  18.1 0.0 copy-start.2
  18.1 0.0 collective-permute-done.3.rest_4_
  18.1 0.0 copy-start.3
  18.1 6.3 %collective-permute-done.4.rest_5_ = bf16[8,32,256]{2,1,0:T(8,128)(2,1)S(1)} collective-permute-done((bf16[8,32,256]{2,1,0:T(8,128)(2,1)}, bf16[8,32,256]{2,1,0:T(8,128)(2,1)S(1)}, u32[]{:S(2)}, u32[]{:S(2)}) %collective-permute-start.4) | collective-permute-done | bytes 131104 | tf_op jit(solution)/shard_map/ppermute | solution.py:426
  24.4 0.0 copy-start.4
  24.4 0.0 collective-permute-done.5.rest_6_
  24.4 0.0 copy-start.5
  24.4 0.0 collective-permute-done.6.rest_7_
  24.4 0.0 copy-start.6
  24.4 0.0 copy-done
  24.5 0.0 copy-done.1
  24.5 0.0 copy-done.2
  24.5 0.0 copy-done.3
  24.5 0.6 copy-done.4
  25.1 0.1 copy-done.5
  25.1 0.0 copy-done.6
  25.2 2.5 %bands.1 = (bf16[2,256,256]{2,1,0:T(8,128)(2,1)}, bf16[2,256,256]{2,1,0:T(8,128)(2,1)}) custom-call(s32[1]{0:T(128)} %bitcast.2.place_ref, bf16[8,32,256]{2,1,0:T(8,128)(2,1)} %get-tuple-element.15.rest_0_, bf16[8,32,256]{2,1,0:T(8,128)(2,1)} %copy-done, bf16[8,32,256]{2,1,0:T(8,128)(2,1)} %copy-done.1, bf16[8,32,256]{2,1,0:T(8,128)(2,1)} %copy-done.2, ...), custom_call_target="tpu_custom_call" | custom-call | bytes 1572864 | tf_op jit(solution)/shard_map/bands/pallas_call | solution.py:306
  27.6 2.9 %collective-permute-start.11 = (bf16[2,256,256]{2,1,0:T(8,128)(2,1)}, bf16[2,256,256]{2,1,0:T(8,128)(2,1)S(1)}, u32[]{:S(2)}, u32[]{:S(2)}) collective-permute-start(bf16[2,256,256]{2,1,0:T(8,128)(2,1)} %get-tuple-element.23.refs_0_.rest_0_), channel_id=1, source_target_pairs={{0,16},{8,24},{16,0},{24,8},{1,17},{9,25},{17,1},{25,9},{2,18},{10... | collective-permute-start | bytes 786440 | tf_op jit(solution)/shard_map/ppermute | solution.py:439
  30.5 0.6 pad_add_fusion.place_ref
  31.2 2.6 %left.1.left_ref = bf16[2,4,256,256]{3,2,1,0:T(8,128)(2,1)} custom-call(bf16[2,256,256]{2,1,0:T(8,128)(2,1)} %get-tuple-element.23.refs_0_.rest_0_, bf16[2,256,256]{2,1,0:T(8,128)(2,1)} %get-tuple-element.24.refs_1_.rest_1_), custom_call_target="tpu_custom_call" | custom-call | bytes 1572864 | tf_op jit(solution)/shard_map/left/pallas_call | solution.py:336
  33.8 0.1 collective-permute-start.8
  33.9 1.8 %collective-permute-start.13 = (bf16[2,256,256]{2,1,0:T(8,128)(2,1)}, bf16[2,256,256]{2,1,0:T(8,128)(2,1)S(1)}, u32[]{:S(2)}, u32[]{:S(2)}) collective-permute-start(bf16[2,256,256]{2,1,0:T(8,128)(2,1)} %get-tuple-element.23.refs_0_.rest_0_), channel_id=1, source_target_pairs={{0,8},{8,0},{16,24},{24,16},{1,9},{9,1},{17,25},{25,17},{2,10},{10... | collective-permute-start | bytes 786440 | tf_op jit(solution)/shard_map/ppermute | solution.py:440
  35.7 0.2 collective-permute-start.14
  35.9 0.7 collective-permute-start.10
  36.6 8.8 %correlate.6.rest_1_ = f32[4,8,2,256,1024]{4,3,2,1,0:T(8,128)} custom-call(s32[2]{0:T(128)} %pad_add_fusion.3.place_ref, bf16[2,4,256,256]{3,2,1,0:T(8,128)(2,1)} %left.1.left_ref, bf16[2,256,256]{2,1,0:T(8,128)(2,1)} %get-tuple-element.23.refs_0_.rest_0_, bf16[2,256,256]{2,1,0:T(8,128)(2,1)} %get-tuple-element.24.refs_1_.rest_1_), custom_call_target="tpu_custom_call" | custom-call | flops 2147483648 | bytes 16777216 | tf_op jit(solution)/shard_map/correlate/pallas_call | solution.py:387
  45.4 3.9 %collective-permute-done.11.rest_0_ = bf16[2,256,256]{2,1,0:T(8,128)(2,1)S(1)} collective-permute-done((bf16[2,256,256]{2,1,0:T(8,128)(2,1)}, bf16[2,256,256]{2,1,0:T(8,128)(2,1)S(1)}, u32[]{:S(2)}, u32[]{:S(2)}) %collective-permute-start.11) | collective-permute-done | bytes 262176 | tf_op jit(solution)/shard_map/ppermute | solution.py:439
  49.3 1.4 %collective-permute-start.7 = (bf16[2,256,256]{2,1,0:T(8,128)(2,1)}, bf16[2,256,256]{2,1,0:T(8,128)(2,1)}, u32[]{:S(2)}, u32[]{:S(2)}) collective-permute-start(bf16[2,256,256]{2,1,0:T(8,128)(2,1)} %get-tuple-element.24.refs_1_.rest_1_), channel_id=1, source_target_pairs={{8,16},{16,8},{9,17},{17,9},{10,18},{18,10},{11,19},{19,11},{12,20... | collective-permute-start | bytes 786440 | tf_op jit(solution)/shard_map/ppermute | solution.py:441
  50.7 5.0 %correlate.7.rest_1_ = f32[4,8,2,256,1024]{4,3,2,1,0:T(8,128)} custom-call(s32[2]{0:T(128)} %pad_add_fusion.2.place_ref, bf16[2,4,256,256]{3,2,1,0:T(8,128)(2,1)} %left.1.left_ref, bf16[2,256,256]{2,1,0:T(8,128)(2,1)S(1)} %collective-permute-done.11.rest_0_, f32[4,8,2,256,1024]{4,3,2,1,0:T(8,128)} %correlate.6.rest_1_), custom_call_target="tpu_custom_call", output_to_operand_aliasing={{}: (3, {})} | custom-call | flops 1073741824 | bytes 8388608 | tf_op jit(solution)/shard_map/correlate/pallas_call | solution.py:387
  55.7 0.0 collective-permute-done.8.rest_0_
  55.7 1.3 %collective-permute-start.12 = (bf16[2,256,256]{2,1,0:T(8,128)(2,1)S(1)}, bf16[2,256,256]{2,1,0:T(8,128)(2,1)S(1)}, u32[]{:S(2)}, u32[]{:S(2)}) collective-permute-start(bf16[2,256,256]{2,1,0:T(8,128)(2,1)S(1)} %collective-permute-done.11.rest_0_), channel_id=1, source_target_pairs={{8,0},{16,24},{9,1},{17,25},{10,2},{18,26},{11,3},{19,27},{12,4},{... | collective-permute-start | bytes 786440 | tf_op jit(solution)/shard_map/ppermute | solution.py:442
  57.0 5.0 %correlate.8.rest_2_ = f32[4,8,2,256,1024]{4,3,2,1,0:T(8,128)} custom-call(s32[2]{0:T(128)} %pad_add_fusion.2.place_ref, bf16[2,4,256,256]{3,2,1,0:T(8,128)(2,1)} %left.1.left_ref, bf16[2,256,256]{2,1,0:T(8,128)(2,1)S(1)} %collective-permute-done.8.rest_0_, f32[4,8,2,256,1024]{4,3,2,1,0:T(8,128)} %correlate.7.rest_1_), custom_call_target="tpu_custom_call", output_to_operand_aliasing={{}: (3, {})} | custom-call | flops 1073741824 | bytes 8388608 | tf_op jit(solution)/shard_map/correlate/pallas_call | solution.py:387
  62.0 0.0 collective-permute-done.13.rest_0_
  62.0 1.3 %collective-permute-start.9 = (bf16[2,256,256]{2,1,0:T(8,128)(2,1)S(1)}, bf16[2,256,256]{2,1,0:T(8,128)(2,1)S(1)}, u32[]{:S(2)}, u32[]{:S(2)}) collective-permute-start(bf16[2,256,256]{2,1,0:T(8,128)(2,1)S(1)} %collective-permute-done.8.rest_0_), channel_id=1, source_target_pairs={{8,0},{16,24},{9,1},{17,25},{10,2},{18,26},{11,3},{19,27},{12,4},{... | collective-permute-start | bytes 786440 | tf_op jit(solution)/shard_map/ppermute | solution.py:442
  63.3 0.0 collective-permute-done.14.rest_1_
  63.3 8.8 %correlate.9.rest_2_ = f32[4,8,2,256,1024]{4,3,2,1,0:T(8,128)} custom-call(s32[2]{0:T(128)} %pad_add_fusion.1.place_ref, bf16[2,4,256,256]{3,2,1,0:T(8,128)(2,1)} %left.1.left_ref, bf16[2,256,256]{2,1,0:T(8,128)(2,1)S(1)} %collective-permute-done.13.rest_0_, ...), custom_call_target="tpu_custom_call", output_to_operand_aliasing={{}: (4, {})} | custom-call | flops 2147483648 | bytes 16777216 | tf_op jit(solution)/shard_map/correlate/pallas_call | solution.py:387
  72.1 0.0 collective-permute-done.10.rest_0_
  72.1 0.0 collective-permute-done.12.rest_1_
  72.1 5.0 %correlate.10.rest_2_ = f32[4,8,2,256,1024]{4,3,2,1,0:T(8,128)} custom-call(s32[2]{0:T(128)} %pad_add_fusion.place_ref, bf16[2,4,256,256]{3,2,1,0:T(8,128)(2,1)} %left.1.left_ref, bf16[2,256,256]{2,1,0:T(8,128)(2,1)S(1)} %collective-permute-done.10.rest_0_, bf16[2,256,256]{2,1,0:T(8,128)(2,1)S(1)} %collective-permute-done.12.rest_1_, ...), custom_call_target="tpu_custom_call", output_to_operand_aliasing={{}: (4, {})} | custom-call | flops 1073741824 | bytes 8388608 | tf_op jit(solution)/shard_map/correlate/pallas_call | solution.py:387
  77.1 0.0 collective-permute-done.7.rest_0_
  77.1 0.0 collective-permute-done.9.rest_1_
  77.2 5.0 %correlate.11 = f32[4,8,2,256,1024]{4,3,2,1,0:T(8,128)} custom-call(s32[2]{0:T(128)} %pad_add_fusion.place_ref, bf16[2,4,256,256]{3,2,1,0:T(8,128)(2,1)} %left.1.left_ref, bf16[2,256,256]{2,1,0:T(8,128)(2,1)} %collective-permute-done.7.rest_0_, bf16[2,256,256]{2,1,0:T(8,128)(2,1)S(1)} %collective-permute-done.9.rest_1_, ...), custom_call_target="tpu_custom_call", output_to_operand_aliasing={{}: (4, {})} | custom-call | flops 1073741824 | bytes 8388608 | tf_op jit(solution)/shard_map/correlate/pallas_call | solution.py:387
Async XLA Ops:
  7.5 5.5 %collective-permute-start = (bf16[8,32,256]{2,1,0:T(8,128)(2,1)}, bf16[8,32,256]{2,1,0:T(8,128)(2,1)S(1)}, u32[]{:S(2)}, u32[]{:S(2)}) collective-permute-start(bf16[8,32,256]{2,1,0:T(8,128)(2,1)} %get-tuple-element.16), channel_id=1, source_target_pairs={{0,1},{1,0},{2,3},{3,2},{4,5},{5,4},{6,7},{7,6},{8,9},{9,8},{10,11... | collective-permute-start | bytes 393224 | tf_op jit(solution)/shard_map/ppermute | solution.py:426
  8.0 7.6 %collective-permute-start.1 = (bf16[8,32,256]{2,1,0:T(8,128)(2,1)}, bf16[8,32,256]{2,1,0:T(8,128)(2,1)S(1)}, u32[]{:S(2)}, u32[]{:S(2)}) collective-permute-start(bf16[8,32,256]{2,1,0:T(8,128)(2,1)} %get-tuple-element.17), channel_id=1, source_target_pairs={{0,2},{1,3},{2,0},{3,1},{4,6},{5,7},{6,4},{7,5},{8,10},{9,11},{10,... | collective-permute-start | bytes 393224 | tf_op jit(solution)/shard_map/ppermute | solution.py:426
  10.6 7.5 %collective-permute-start.2 = (bf16[8,32,256]{2,1,0:T(8,128)(2,1)}, bf16[8,32,256]{2,1,0:T(8,128)(2,1)S(1)}, u32[]{:S(2)}, u32[]{:S(2)}) collective-permute-start(bf16[8,32,256]{2,1,0:T(8,128)(2,1)} %get-tuple-element.18), channel_id=1, source_target_pairs={{0,3},{1,2},{2,1},{3,0},{4,7},{5,6},{6,5},{7,4},{8,11},{9,10},{10,... | collective-permute-start | bytes 393224 | tf_op jit(solution)/shard_map/ppermute | solution.py:426
  10.6 7.5 %collective-permute-start.3 = (bf16[8,32,256]{2,1,0:T(8,128)(2,1)}, bf16[8,32,256]{2,1,0:T(8,128)(2,1)S(1)}, u32[]{:S(2)}, u32[]{:S(2)}) collective-permute-start(bf16[8,32,256]{2,1,0:T(8,128)(2,1)} %get-tuple-element.19), channel_id=1, source_target_pairs={{0,4},{1,5},{2,6},{3,7},{4,0},{5,1},{6,2},{7,3},{8,12},{9,13},{10,... | collective-permute-start | bytes 393224 | tf_op jit(solution)/shard_map/ppermute | solution.py:426
  12.4 12.0 %collective-permute-start.4 = (bf16[8,32,256]{2,1,0:T(8,128)(2,1)}, bf16[8,32,256]{2,1,0:T(8,128)(2,1)S(1)}, u32[]{:S(2)}, u32[]{:S(2)}) collective-permute-start(bf16[8,32,256]{2,1,0:T(8,128)(2,1)} %get-tuple-element.20), channel_id=1, source_target_pairs={{0,5},{1,4},{2,7},{3,6},{4,1},{5,0},{6,3},{7,2},{8,13},{9,12},{10,... | collective-permute-start | bytes 393224 | tf_op jit(solution)/shard_map/ppermute | solution.py:426
  13.0 11.4 %copy-start = (bf16[8,32,256]{2,1,0:T(8,128)(2,1)}, bf16[8,32,256]{2,1,0:T(8,128)(2,1)S(1)}, u32[]{:S(2)}) copy-start(bf16[8,32,256]{2,1,0:T(8,128)(2,1)S(1)} %collective-permute-done.rest_1_) | copy-start | bytes 393220
  13.0 11.4 %collective-permute-start.5 = (bf16[8,32,256]{2,1,0:T(8,128)(2,1)}, bf16[8,32,256]{2,1,0:T(8,128)(2,1)S(1)}, u32[]{:S(2)}, u32[]{:S(2)}) collective-permute-start(bf16[8,32,256]{2,1,0:T(8,128)(2,1)} %get-tuple-element.21), channel_id=1, source_target_pairs={{0,6},{1,7},{2,4},{3,5},{4,2},{5,3},{6,0},{7,1},{8,14},{9,15},{10,... | collective-permute-start | bytes 393224 | tf_op jit(solution)/shard_map/ppermute | solution.py:426
  15.7 8.8 %copy-start.1 = (bf16[8,32,256]{2,1,0:T(8,128)(2,1)}, bf16[8,32,256]{2,1,0:T(8,128)(2,1)S(1)}, u32[]{:S(2)}) copy-start(bf16[8,32,256]{2,1,0:T(8,128)(2,1)S(1)} %collective-permute-done.1.rest_2_) | copy-start | bytes 393220
  15.7 8.8 %collective-permute-start.6 = (bf16[8,32,256]{2,1,0:T(8,128)(2,1)}, bf16[8,32,256]{2,1,0:T(8,128)(2,1)S(1)}, u32[]{:S(2)}, u32[]{:S(2)}) collective-permute-start(bf16[8,32,256]{2,1,0:T(8,128)(2,1)} %get-tuple-element.22), channel_id=1, source_target_pairs={{0,7},{1,6},{2,5},{3,4},{4,3},{5,2},{6,1},{7,0},{8,15},{9,14},{10,... | collective-permute-start | bytes 393224 | tf_op jit(solution)/shard_map/ppermute | solution.py:426
  18.1 6.4 %copy-start.2 = (bf16[8,32,256]{2,1,0:T(8,128)(2,1)}, bf16[8,32,256]{2,1,0:T(8,128)(2,1)S(1)}, u32[]{:S(2)}) copy-start(bf16[8,32,256]{2,1,0:T(8,128)(2,1)S(1)} %collective-permute-done.2.rest_3_) | copy-start | bytes 393220
  18.1 6.4 %copy-start.3 = (bf16[8,32,256]{2,1,0:T(8,128)(2,1)}, bf16[8,32,256]{2,1,0:T(8,128)(2,1)S(1)}, u32[]{:S(2)}) copy-start(bf16[8,32,256]{2,1,0:T(8,128)(2,1)S(1)} %collective-permute-done.3.rest_4_) | copy-start | bytes 393220
  24.4 0.6 copy-start.4
  24.4 0.7 copy-start.5
  24.4 0.7 copy-start.6
  27.6 21.7 %collective-permute-start.11 = (bf16[2,256,256]{2,1,0:T(8,128)(2,1)}, bf16[2,256,256]{2,1,0:T(8,128)(2,1)S(1)}, u32[]{:S(2)}, u32[]{:S(2)}) collective-permute-start(bf16[2,256,256]{2,1,0:T(8,128)(2,1)} %get-tuple-element.23.refs_0_.rest_0_), channel_id=1, source_target_pairs={{0,16},{8,24},{16,0},{24,8},{1,17},{9,25},{17,1},{25,9},{2,18},{10... | collective-permute-start | bytes 786440 | tf_op jit(solution)/shard_map/ppermute | solution.py:439
  33.8 21.9 %collective-permute-start.8 = (bf16[2,256,256]{2,1,0:T(8,128)(2,1)}, bf16[2,256,256]{2,1,0:T(8,128)(2,1)S(1)}, u32[]{:S(2)}, u32[]{:S(2)}) collective-permute-start(bf16[2,256,256]{2,1,0:T(8,128)(2,1)} %get-tuple-element.24.refs_1_.rest_1_), channel_id=1, source_target_pairs={{0,16},{8,24},{16,0},{24,8},{1,17},{9,25},{17,1},{25,9},{2,18},{10... | collective-permute-start | bytes 786440 | tf_op jit(solution)/shard_map/ppermute | solution.py:439
  33.9 28.1 %collective-permute-start.13 = (bf16[2,256,256]{2,1,0:T(8,128)(2,1)}, bf16[2,256,256]{2,1,0:T(8,128)(2,1)S(1)}, u32[]{:S(2)}, u32[]{:S(2)}) collective-permute-start(bf16[2,256,256]{2,1,0:T(8,128)(2,1)} %get-tuple-element.23.refs_0_.rest_0_), channel_id=1, source_target_pairs={{0,8},{8,0},{16,24},{24,16},{1,9},{9,1},{17,25},{25,17},{2,10},{10... | collective-permute-start | bytes 786440 | tf_op jit(solution)/shard_map/ppermute | solution.py:440
  35.7 27.6 %collective-permute-start.14 = (bf16[2,256,256]{2,1,0:T(8,128)(2,1)}, bf16[2,256,256]{2,1,0:T(8,128)(2,1)S(1)}, u32[]{:S(2)}, u32[]{:S(2)}) collective-permute-start(bf16[2,256,256]{2,1,0:T(8,128)(2,1)} %get-tuple-element.24.refs_1_.rest_1_), channel_id=1, source_target_pairs={{0,8},{8,0},{16,24},{24,16},{1,9},{9,1},{17,25},{25,17},{2,10},{10... | collective-permute-start | bytes 786440 | tf_op jit(solution)/shard_map/ppermute | solution.py:440
  35.9 36.2 %collective-permute-start.10 = (bf16[2,256,256]{2,1,0:T(8,128)(2,1)}, bf16[2,256,256]{2,1,0:T(8,128)(2,1)S(1)}, u32[]{:S(2)}, u32[]{:S(2)}) collective-permute-start(bf16[2,256,256]{2,1,0:T(8,128)(2,1)} %get-tuple-element.23.refs_0_.rest_0_), channel_id=1, source_target_pairs={{8,16},{16,8},{9,17},{17,9},{10,18},{18,10},{11,19},{19,11},{12,20... | collective-permute-start | bytes 786440 | tf_op jit(solution)/shard_map/ppermute | solution.py:441
  49.3 27.8 %collective-permute-start.7 = (bf16[2,256,256]{2,1,0:T(8,128)(2,1)}, bf16[2,256,256]{2,1,0:T(8,128)(2,1)}, u32[]{:S(2)}, u32[]{:S(2)}) collective-permute-start(bf16[2,256,256]{2,1,0:T(8,128)(2,1)} %get-tuple-element.24.refs_1_.rest_1_), channel_id=1, source_target_pairs={{8,16},{16,8},{9,17},{17,9},{10,18},{18,10},{11,19},{19,11},{12,20... | collective-permute-start | bytes 786440 | tf_op jit(solution)/shard_map/ppermute | solution.py:441
  55.7 16.4 %collective-permute-start.12 = (bf16[2,256,256]{2,1,0:T(8,128)(2,1)S(1)}, bf16[2,256,256]{2,1,0:T(8,128)(2,1)S(1)}, u32[]{:S(2)}, u32[]{:S(2)}) collective-permute-start(bf16[2,256,256]{2,1,0:T(8,128)(2,1)S(1)} %collective-permute-done.11.rest_0_), channel_id=1, source_target_pairs={{8,0},{16,24},{9,1},{17,25},{10,2},{18,26},{11,3},{19,27},{12,4},{... | collective-permute-start | bytes 786440 | tf_op jit(solution)/shard_map/ppermute | solution.py:442
  62.0 15.1 %collective-permute-start.9 = (bf16[2,256,256]{2,1,0:T(8,128)(2,1)S(1)}, bf16[2,256,256]{2,1,0:T(8,128)(2,1)S(1)}, u32[]{:S(2)}, u32[]{:S(2)}) collective-permute-start(bf16[2,256,256]{2,1,0:T(8,128)(2,1)S(1)} %collective-permute-done.8.rest_0_), channel_id=1, source_target_pairs={{8,0},{16,24},{9,1},{17,25},{10,2},{18,26},{11,3},{19,27},{12,4},{... | collective-permute-start | bytes 786440 | tf_op jit(solution)/shard_map/ppermute | solution.py:442

commit v2 on v1

v2 whole, which is shorter than its diff:
```python
import functools
import math

import jax
import jax.numpy as jnp
import numpy as np
from jax import lax
from jax.experimental import pallas as pl
from jax.experimental.pallas import tpu as pltpu
from jax.sharding import PartitionSpec as P

AVG = 16
LANES = 128
HALVES = 2
SLOTS_OUT = 4


def shifted(block, axis, distance):
    devices = range(lax.axis_size(axis))
    route = [(i - distance, i) for i in devices if i - distance in devices]
    return lax.ppermute(block, axis, route)


def rotation(numbers, modulus):
    angles = (numbers % modulus).astype(jnp.float32) * jnp.float32(-2.0 * math.pi / modulus)
    return (jnp.cos(angles), jnp.sin(angles))


def split_pair(table):
    upper = table.astype(jnp.bfloat16)
    lower = (table - upper.astype(jnp.float32)).astype(jnp.bfloat16)
    return (upper, lower)


def complex_table(real_part, imag_part, axis_at):
    first = jnp.stack([real_part, imag_part], axis=-1)
    second = jnp.stack([-imag_part, real_part], axis=-1)
    return jnp.stack([first, second], axis=axis_at)


def all_frames(voltages, fir_taps):
    inputs_dev, _, frames_dev, slot_count = voltages.shape
    phases = fir_taps.shape[0]
    tap_count = fir_taps.shape[1]
    lane_count = lax.axis_size("chan")
    groups = lane_count // phases
    position = lax.axis_index("chan")
    my_phase = position % phases
    my_group = position // phases
    recent = voltages[:, 0]
    if groups > 1:
        earlier = shifted(voltages[:, 0, frames_dev - (tap_count - 1) :, :], "chan", phases)
    else:
        earlier = jnp.zeros((inputs_dev, tap_count - 1, slot_count), voltages.dtype)
    series = jnp.concatenate([earlier, recent], axis=1)
    coeffs = lax.dynamic_index_in_dim(fir_taps, my_phase, 0, keepdims=False)
    frame_ids = my_group * frames_dev + jnp.arange(frames_dev, dtype=jnp.int32)
    keep_mask = (frame_ids >= tap_count - 1).astype(jnp.float32)
    filtered = sum(
        (
            coeffs[tap_index]
            * series[:, tap_count - 1 - tap_index : tap_count - 1 - tap_index + frames_dev].astype(
                jnp.float32
            )
            for tap_index in range(tap_count)
        )
    )
    filtered = filtered * keep_mask[None, :, None]
    better = lax.Precision.HIGH
    split_len = slot_count // phases
    folded = filtered.reshape(inputs_dev, frames_dev, split_len, phases)
    slot_ids = jnp.arange(split_len, dtype=jnp.int32)
    short_re, short_im = rotation(slot_ids[:, None] * slot_ids[None, :], split_len)
    short_table = jnp.stack([short_re, short_im], axis=-1)
    inner = jnp.einsum(
        "ifqr,qvc->rvcfi", folded, short_table, precision=better, preferred_element_type=jnp.float32
    )
    rest_ids = jnp.arange(phases, dtype=jnp.int32)
    freq_ids = jnp.arange(slot_count, dtype=jnp.int32).reshape(phases, split_len)
    twist_re, twist_im = rotation(
        (my_phase + phases * rest_ids)[:, None, None] * freq_ids[None], phases * slot_count
    )
    twist_table = complex_table(twist_re, twist_im, 3)
    branch = jnp.einsum(
        "rvcfi,ruvcd->uvfdi",
        inner,
        twist_table,
        precision=better,
        preferred_element_type=jnp.float32,
    )
    branch = branch.reshape(slot_count, 1, frames_dev, 2, inputs_dev).astype(jnp.bfloat16)
    band_count = phases // 2
    band_re, band_im = rotation(
        rest_ids[:, None] * jnp.arange(band_count, dtype=jnp.int32)[None, :], phases
    )
    band_table = complex_table(band_re, band_im, 1)
    band_upper, band_lower = split_pair(band_table)
    turned = lax.all_to_all(branch, "chan", split_axis=0, concat_axis=1, tiled=True)
    span_len = turned.shape[0]
    sources = turned.shape[1]
    item_count = turned.shape[2]
    grouped = turned.reshape(span_len, sources // phases, phases, item_count, 2, inputs_dev)
    phase_form = "wgpfci,pcbd->bwgfdi"
    total = jnp.einsum(
        phase_form, grouped, band_upper, preferred_element_type=jnp.float32
    ) + jnp.einsum(phase_form, grouped, band_lower, preferred_element_type=jnp.float32)
    spectra = total.astype(jnp.bfloat16)
    span_dev = spectra.shape[1]
    subs_dev = span_dev // AVG
    stacked = spectra.reshape(band_count, subs_dev, AVG * groups * frames_dev, 2, inputs_dev)
    columns = stacked.reshape(band_count, subs_dev, -1, inputs_dev)
    swapped = jnp.stack([stacked[:, :, :, 1], -stacked[:, :, :, 0]], axis=3).reshape(
        band_count, subs_dev, -1, inputs_dev
    )
    left_side = jnp.stack([columns, swapped], axis=2)
    spectra_count = groups * frames_dev - (tap_count - 1)
    scaling = 1.0 / (phases * slot_count * AVG * spectra_count)
    vis_form = "bsokn,bskw->bsonw"
    return (
        jnp.einsum(
            vis_form,
            left_side,
            lax.all_gather(columns, "stn", axis=3, tiled=True),
            preferred_element_type=jnp.float32,
        )
        * scaling
    )


def split_value(value):
    upper = value.astype(jnp.bfloat16)
    lower = (value - upper.astype(jnp.float32)).astype(jnp.bfloat16)
    return upper, lower


def weighted(terms, weights):
    total = None
    for term, weight in zip(terms, weights):
        if abs(weight) < 1e-9:
            continue
        part = term if abs(abs(weight) - 1.0) < 1e-9 else term * jnp.float32(abs(weight))
        if total is None:
            total = -part if weight < 0 else part
        else:
            total = total - part if weight < 0 else total + part
    return total


def turn_weights(count, step, radix):
    angles = [-2.0 * math.pi * ((k * step) % radix) / radix for k in range(count)]
    return [math.cos(a) for a in angles], [math.sin(a) for a in angles]


def half_sums(pieces):
    half = len(pieces) // 2
    sums = [pieces[k] + pieces[k + half] for k in range(half)]
    differences = [pieces[k] - pieces[k + half] for k in range(half)]
    return sums, differences


def branch_tables(phases, radix, dests):
    slots = radix * LANES
    near = LANES // dests
    rows = near // HALVES
    entry = np.arange(LANES).reshape(dests, HALVES, rows).transpose(1, 0, 2)
    v = np.repeat(entry[:, :, None], 2, axis=2).reshape(-1, 1)
    is_imag = np.broadcast_to(np.arange(2)[:, None], (HALVES, dests, 2, rows)).reshape(-1, 1)
    column = np.arange(2 * LANES)[None, :]
    b, half = column % LANES, column // LANES
    angle = -2.0 * np.pi * ((v * b) % LANES) / LANES + 0.5 * np.pi * (half - is_imag)
    far = np.stack([np.cos(angle), np.sin(angle)])
    phase = np.arange(phases)
    angle = -2.0 * np.pi * ((v * phase[None, :]) % slots) / slots
    row = np.stack([np.cos(angle), np.sin(angle)], axis=1).transpose(2, 0, 1)
    row = np.broadcast_to(row[..., None], row.shape + (1,))
    u = np.arange(radix)[None, :, None]
    turns = (u * (phase[:, None, None] + phases * b[None])) % (phases * slots)
    angle = -2.0 * np.pi * turns / (phases * slots)
    low = np.stack([np.cos(angle), np.sin(angle)], axis=1)
    mirrored = (u > radix // 2) & (half[None] == 1)
    low = np.where(mirrored[:, None], -low, low)
    return far.astype(np.float32), row[..., 0].astype(np.float32), low.astype(np.float32)


def table_copies(half, me, far_ref, row_ref, low_ref, far, row, low, sems):
    rows = pl.ds(half * far.shape[1], far.shape[1])
    pairs = ((far_ref.at[:, rows], far), (row_ref.at[me, rows], row), (low_ref.at[me], low))
    return [pltpu.make_async_copy(source, target, sems.at[i]) for i, (source, target) in enumerate(pairs)]


def make_table(me, dests, far, row, low, table):
    share = far.shape[1] // dests
    for k in range(dests):
        at = pl.ds(pl.multiple_of(lax.bitwise_xor(me, k) * share, share), share)
        row_cos, row_sin = row[at, 0:1], row[at, 1:2]
        far_cos = far[0, at] * row_cos - far[1, at] * row_sin
        far_sin = far[0, at] * row_sin + far[1, at] * row_cos
        for u in range(table.shape[1]):
            entry = far_cos * low[0, u : u + 1] - far_sin * low[1, u : u + 1]
            to = pl.ds(k * share, share)
            table[0, u, to], table[1, u, to] = split_value(entry)


def transform(table, y, outs):
    radix = table.shape[1]
    share = table.shape[2] // len(outs)
    for u in range(radix):
        source = min(u, radix - u)
        total = jnp.dot(table[0, u], y[source, 0], preferred_element_type=jnp.float32)
        total += jnp.dot(table[0, u], y[source, 1], preferred_element_type=jnp.float32)
        total += jnp.dot(table[1, u], y[source, 0], preferred_element_type=jnp.float32)
        total = total.astype(jnp.bfloat16)
        for k, out_ref in enumerate(outs):
            out_ref[u] = total[k * share : (k + 1) * share]


def first_kernel(radix, dests, place_ref, volt_ref, taps_ref, far_ref, row_ref, low_ref, *rest):
    outs = rest[:dests]
    y, volts, filtered, table, taps, far, row, low, volt_sems, sems = rest[dests:]
    me = place_ref[0]
    parts, rows = volts.shape[0], volts.shape[1]
    small = table_copies(0, me, far_ref, row_ref, low_ref, far, row, low, sems)
    small.append(pltpu.make_async_copy(taps_ref.at[me], taps, sems.at[3]))
    loads = [
        pltpu.make_async_copy(volt_ref.at[pl.ds(i * rows, rows), 0], volts.at[i], volt_sems.at[i])
        for i in range(parts)
    ]
    for load in small + loads:
        load.start()
    for load in small:
        load.wait()
    make_table(me, dests, far, row, low, table)
    by_frame = jnp.concatenate([taps[k : k + 1] for k in reversed(range(taps.shape[0]))], axis=0)
    together = LANES // rows
    for i, load in enumerate(loads):
        load.wait()
        filtered[pl.ds(i * rows, rows)] = jnp.sum(volts[i].astype(jnp.float32) * by_frame[None], axis=1)
        if (i + 1) % together:
            continue
        inputs = pl.ds((i + 1) * rows - LANES, LANES)
        pieces = [filtered[inputs, a * LANES : (a + 1) * LANES].T for a in range(radix)]
        sums, differences = half_sums(pieces)
        for u in range(radix // 2 + 1):
            terms = differences if u % 2 else sums
            for part, weights in enumerate(turn_weights(radix // 2, u, radix)):
                value = weighted(terms, weights)
                if value is None:
                    value = jnp.zeros_like(pieces[0])
                at = (pl.ds(part * LANES, LANES), inputs)
                y[(u, 0) + at], y[(u, 1) + at] = split_value(value)
    transform(table, y, outs)


def next_kernel(half, dests, place_ref, y, far_ref, row_ref, low_ref, *rest):
    outs = rest[:dests]
    table, far, row, low, sems = rest[dests:]
    me = place_ref[0]
    small = table_copies(half, me, far_ref, row_ref, low_ref, far, row, low, sems)
    for load in small:
        load.start()
    for load in small:
        load.wait()
    make_table(me, dests, far, row, low, table)
    transform(table, y, outs)


def branch_of(voltages, fir_taps, me, dests):
    inputs, _, frames, slots = voltages.shape
    phases, tap_count, _ = fir_taps.shape
    radix = slots // LANES
    rows = LANES // dests // HALVES
    far, row, low = branch_tables(phases, radix, dests)
    parts = 8
    here = far.shape[1] // HALVES
    whole, near = pl.BlockSpec(memory_space=pl.ANY), pl.BlockSpec(memory_space=pltpu.VMEM)
    place = pl.BlockSpec(memory_space=pltpu.SMEM)
    blocks = [pltpu.VMEM((radix, 2 * rows, inputs), jnp.bfloat16)] * dests
    y = pltpu.VMEM((radix // 2 + 1, 2, 2 * LANES, inputs), jnp.bfloat16)
    table = pltpu.VMEM((2, radix, here, 2 * LANES), jnp.bfloat16)
    small = [
        pltpu.VMEM((2, here, 2 * LANES), jnp.float32),
        pltpu.VMEM((here, row.shape[2]), jnp.float32),
        pltpu.VMEM(low.shape[1:], jnp.float32),
    ]
    flops = 6 * radix * inputs * 2 * LANES * here
    *first, y = pl.pallas_call(
        functools.partial(first_kernel, radix, dests),
        out_shape=blocks + [y],
        in_specs=[place] + [whole] * 5,
        out_specs=[near] * (dests + 1),
        scratch_shapes=[
            pltpu.VMEM((parts, inputs // parts, frames, slots), jnp.bfloat16),
            pltpu.VMEM((inputs, slots), jnp.float32),
            table,
            pltpu.VMEM((tap_count, slots), jnp.float32),
        ]
        + small
        + [pltpu.SemaphoreType.DMA((parts,)), pltpu.SemaphoreType.DMA((4,))],
        cost_estimate=pl.CostEstimate(flops=flops, transcendentals=0, bytes_accessed=2 * voltages.size),
        name="branch",
    )(me.reshape(1), voltages, fir_taps, far, row, low)
    y = near_memory(y)
    result = [first]
    for half in range(1, HALVES):
        result.append(
            pl.pallas_call(
                functools.partial(next_kernel, half, dests),
                out_shape=blocks,
                in_specs=[place, near] + [whole] * 3,
                out_specs=[near] * dests,
                scratch_shapes=[table] + small + [pltpu.SemaphoreType.DMA((3,))],
                cost_estimate=pl.CostEstimate(flops=flops, transcendentals=0, bytes_accessed=4 * far.size),
                name="branch_next",
            )(me.reshape(1), y, far, row, low)
        )
    return [[near_memory(x) for x in part] for part in result]


def band_kernel(place_ref, *rest):
    out_ref, turned, sems = rest[-3:]
    phases, radix, rows, _ = turned.shape
    blocks = rest[:phases]
    me = place_ref[0]
    loads = [
        pltpu.make_async_copy(blocks[k], turned.at[lax.bitwise_xor(me, k)], sems.at[k]) for k in range(phases)
    ]
    for load in loads:
        load.start()
    for load in loads:
        load.wait()
    near = rows // 2
    for u in range(radix):
        pair = [turned[p, u].astype(jnp.float32) for p in range(phases)]
        re_pair, im_pair = half_sums([x[:near] for x in pair]), half_sums([x[near:] for x in pair])
        for c in range(phases // 2):
            cos_w, sin_w = turn_weights(phases // 2, c, phases)
            terms = re_pair[c % 2] + im_pair[c % 2]
            spectrum = [weighted(terms, cos_w + [-w for w in sin_w]), weighted(terms, sin_w + cos_w)]
            out_ref[c, u * rows : (u + 1) * rows] = jnp.concatenate(spectrum, axis=0).astype(jnp.bfloat16)


def bands_of(blocks, me):
    phases = len(blocks)
    radix, rows, inputs = blocks[0].shape
    bands, depth = phases // 2, radix * rows
    return pl.pallas_call(
        band_kernel,
        out_shape=pltpu.VMEM((bands, depth, inputs), jnp.bfloat16),
        in_specs=[pl.BlockSpec(memory_space=pltpu.SMEM)] + [pl.BlockSpec(memory_space=pltpu.VMEM)] * phases,
        out_specs=pl.BlockSpec(memory_space=pltpu.VMEM),
        scratch_shapes=[
            pltpu.VMEM((phases, radix, rows, inputs), jnp.bfloat16),
            pltpu.SemaphoreType.DMA((phases,)),
        ],
        cost_estimate=pl.CostEstimate(flops=0, transcendentals=0, bytes_accessed=6 * bands * depth * inputs),
        name="bands",
    )(me.reshape(1), *blocks)


def left_kernel(near, right_ref, left_ref):
    for c in range(left_ref.shape[1]):
        turned = right_ref[c].astype(jnp.float32).T
        left_ref[0, c] = turned.astype(jnp.bfloat16)
        depth = turned.shape[1]
        real = lax.broadcasted_iota(jnp.int32, turned.shape, 1) % (2 * near) < near
        ahead = pltpu.roll(turned, depth - near, 1)
        behind = pltpu.roll(turned, near, 1)
        left_ref[1, c] = jnp.where(real, ahead, -behind).astype(jnp.bfloat16)


def left_of(right, near):
    bands, depth, inputs = right.shape
    return pl.pallas_call(
        functools.partial(left_kernel, near),
        out_shape=pltpu.VMEM((2, bands, inputs, depth), jnp.bfloat16),
        in_specs=[pl.BlockSpec(memory_space=pltpu.VMEM)],
        out_specs=pl.BlockSpec(memory_space=pltpu.VMEM),
        cost_estimate=pl.CostEstimate(flops=0, transcendentals=0, bytes_accessed=6 * bands * depth * inputs),
        name="left",
    )(right)


def correlate_kernel(near, group, jobs, scaling, me_ref, *rest):
    out_ref, buffer, sems = rest[-3:]
    halves = sorted({job[0] for job in jobs})
    lefts, rights = dict(zip(halves, rest)), rest[len(halves) :]
    slots, block, _, _, width = buffer.shape
    bands, depth = rest[0].shape[1], rest[0].shape[3]
    subs = near // group
    pieces = subs // block
    count = bands * pieces
    lanes = lax.broadcasted_iota(jnp.int32, (16, depth), 1) % near // group
    stations = out_ref.shape[-1] // width

    for at, (half, back) in enumerate(jobs):
        source = lax.rem(me_ref[0] + (stations - back), stations)
        columns = pl.ds(pl.multiple_of(source * width, width), width)

        def store(band, piece, slot):
            to = out_ref.at[band, pl.ds(half * subs + piece * block, block), :, :, columns]
            return pltpu.make_async_copy(buffer.at[slot], to, sems.at[slot])

        def item(i, _):
            band, piece, slot = i // pieces, i % pieces, (at * count + i) % slots

            @pl.when(at * count + i >= slots)
            def _():
                store(0, 0, slot).wait()

            right = rights[at][band]
            for k in range(block):
                mask = (lanes == piece * block + k).astype(jnp.float32).astype(jnp.bfloat16)[:1]
                for part in range(2):
                    product = jnp.dot(lefts[half][part, band] * mask, right, preferred_element_type=jnp.float32)
                    buffer[slot, k, part] = product * scaling
            store(band, piece, slot).start()
            return 0

        lax.fori_loop(0, count, item, 0)
    for slot in range(slots):
        store(0, 0, slot).wait()


def correlate(lefts, jobs, me, total, near, radix, scaling, shape):
    _, bands, inputs, depth = lefts[0].shape
    needed = [lefts[half] for half in sorted({job[0] for job in jobs})]
    group = AVG // radix
    block = math.gcd(near // group, 2)
    fresh = total is None
    flat = [array for _, _, array in jobs]
    listed = tuple((half, back) for half, back, _ in jobs)
    return pl.pallas_call(
        functools.partial(correlate_kernel, near, group, listed, scaling),
        out_shape=jax.ShapeDtypeStruct(shape, jnp.float32),
        in_specs=[pl.BlockSpec(memory_space=pltpu.SMEM)]
        + [pl.BlockSpec(memory_space=pltpu.VMEM)] * (len(needed) + len(flat))
        + ([] if fresh else [pl.BlockSpec(memory_space=pl.ANY)]),
        out_specs=pl.BlockSpec(memory_space=pl.ANY),
        scratch_shapes=[
            pltpu.VMEM((SLOTS_OUT, block, 2, inputs, inputs), jnp.float32),
            pltpu.SemaphoreType.DMA((SLOTS_OUT,)),
        ],
        input_output_aliases={} if fresh else {1 + len(needed) + len(flat): 0},
        cost_estimate=pl.CostEstimate(
            flops=4 * len(jobs) * bands * near // group * inputs * inputs * depth,
            transcendentals=0,
            bytes_accessed=8 * len(jobs) * bands * near // group * inputs * inputs,
        ),
        name="correlate",
    )(*([me.reshape(1)] + needed + flat + ([] if fresh else [total])))


def near_memory(array):
    return pltpu.with_memory_space_constraint(array, pltpu.VMEM)


def one_frame(voltages, fir_taps):
    inputs, _, _, slots = voltages.shape
    phases = fir_taps.shape[0]
    dests = lax.axis_size("chan")
    radix = slots // LANES
    near = LANES // dests // HALVES
    place = lax.axis_index("chan")
    branch = branch_of(voltages, fir_taps, place, dests)
    own, lefts = [], []
    for h in range(HALVES):
        blocks = list(branch[h])
        for k in range(1, dests):
            route = [(i, i ^ k) for i in range(dests)]
            blocks[k] = near_memory(lax.ppermute(blocks[k], "chan", route))
        own.append(near_memory(bands_of(blocks, place)))
        lefts.append(near_memory(left_of(own[h], near)))
    me = lax.axis_index("stn")
    stations = lax.axis_size("stn")
    shape = (phases // 2, HALVES * near * radix // AVG, 2, inputs, inputs * stations)
    scaling = 1.0 / (phases * slots * AVG)
    add = functools.partial(correlate, lefts, me=me, near=near, radix=radix, scaling=scaling, shape=shape)
    onward = [(i, (i + 1) % stations) for i in range(stations)]
    backward = [(i, (i - 1) % stations) for i in range(stations)]
    first, last, second = [], [], []
    for h, x in enumerate(own):
        first.append(near_memory(lax.ppermute(x, "stn", onward)))
        last.append(near_memory(lax.ppermute(x, "stn", backward)))
        second.append(near_memory(lax.ppermute(first[h], "stn", onward)))
    total = add([(0, 0, own[0])], total=None)
    total = add([(1, 0, own[1]), (0, 1, first[0]), (0, 3, last[0])], total=total)
    total = add([(0, 2, second[0]), (1, 1, first[1])], total=total)
    total = add([(1, 3, last[1])], total=total)
    total = add([(1, 2, second[1])], total=total)
    return total


def per_device(voltages, fir_taps):
    inputs, _, frames, slots = voltages.shape
    phases, tap_count, _ = fir_taps.shape
    lanes = lax.axis_size("chan")
    radix = slots // LANES
    fits = (
        lanes == phases
        and frames == tap_count
        and phases & (phases - 1) == 0
        and phases % 2 == 0
        and slots % LANES == 0
        and radix % 2 == 0
        and AVG % radix == 0
        and LANES % (8 * HALVES * lanes) == 0
        and lax.axis_size("stn") == 4
        and inputs % LANES == 0
    )
    return one_frame(voltages, fir_taps) if fits else all_frames(voltages, fir_taps)


def solution(mesh):
    return jax.shard_map(
        per_device,
        mesh=mesh,
        in_specs=(P("stn", "chan", None, None), P()),
        out_specs=P(None, "chan", None, "stn", None),
        check_vma=False,
    )
```

time: 83.1 us -> 69.7 us (0.84)
  Pallas kernels: 50.2 us -> 36 us
  starting transfers between devices: 18.3 us -> 28.1 us
  waiting for transfers between devices: 10.3 us -> 5.33 us
  other arithmetic: 2.55 us -> 0 us
    pallas_call x9 -> x11, Pallas kernels: 50.2 us -> 36 us  [the longest x5 25.7 us: correlate(): pl.pallas_call(functools.partial(correlate_kernel, near, group, listed, s...]
    ppermute x15 -> x20, starting transfers between devices: 18.3 us -> 28.1 us  [the longest x14 15.7 us: one_frame(): blocks[k] = near_memory(lax.ppermute(blocks[k], 'chan', route))]
    ppermute x15 -> x20, waiting for transfers between devices: 10.3 us -> 5.33 us  [the longest x14 3.63 us: one_frame(): blocks[k] = near_memory(lax.ppermute(blocks[k], 'chan', route))]
    another operation x4 -> x0, other arithmetic: 2.55 us -> none  [spot(): return jnp.stack([me ^ k, inner.astype(jnp.int32)])]
  transfers between devices with their start and end apart: 15 -> 20, of which waited for: 2 -> 4; matrix products, arithmetic and copies ran while one was open for 3% -> 0% of each run, Pallas kernels for 43% -> 38%
where the time goes in v2:
time: 69.7 us; the launch traced here: 69.5 us
  Pallas kernels  36 us (52%)
  starting transfers between devices  28.1 us (40%)
  waiting for transfers between devices  5.33 us (8%)
    pallas_call x5, Pallas kernels, correlate(): pl.pallas_call(functools.partial(correlate_kernel, near, group, listed, s...  25.7 us
    ppermute x14, starting transfers between devices, one_frame(): blocks[k] = near_memory(lax.ppermute(blocks[k], 'chan', route))  15.7 us
    pallas_call x1, Pallas kernels, branch_of(): pl.pallas_call(functools.partial(first_kernel, radix, dests), out_shape=b...  6.15 us
    ppermute x2, starting transfers between devices, one_frame(): last.append(near_memory(lax.ppermute(x, 'stn', backward)))  6.12 us
    ppermute x14, waiting for transfers between devices, one_frame(): blocks[k] = near_memory(lax.ppermute(blocks[k], 'chan', route))  3.63 us
    ppermute x2, starting transfers between devices, one_frame(): first.append(near_memory(lax.ppermute(x, 'stn', onward)))  3.26 us
    ppermute x2, starting transfers between devices, one_frame(): second.append(near_memory(lax.ppermute(first[h], 'stn', onward)))  2.99 us
    pallas_call x2, Pallas kernels, bands_of(): pl.pallas_call(band_kernel, out_shape=pltpu.VMEM((bands, depth, inputs),...  1.8 us
  transfers between devices with their start and end apart: 20, of which 4 were waited for; matrix products, arithmetic and copies ran while one was open for 0% of the time, Pallas kernels for 38%

profile of v2, /device:TPU:0, one launch (start us, length us, event | category | flops | bytes accessed | tf_op | source)
XLA Modules:
  0.0 69.5 jit_solution(10853219312567896798)
XLA Ops:
  0.0 6.2 %branch.1 = (bf16[8,16,256]{2,1,0:T(8,128)(2,1)S(1)}, bf16[8,16,256]{2,1,0:T(8,128)(2,1)S(1)}, bf16[8,16,256]{2,1,0:T(8,128)(2,1)S(1)}, bf16[8,16,256]{2,1,0:T(8...) custom-call(s32[1]{0:T(128)} %bitcast.1.place_ref, ...), custom_call_target="tpu_custom_call" | custom-call | flops 402653184 | bytes 4194304 | tf_op jit(solution)/shard_map/branch/pallas_call | solution.py:286
  6.2 0.6 collective-permute-start.10
  6.7 2.5 %collective-permute-start.11 = (bf16[8,16,256]{2,1,0:T(8,128)(2,1)S(1)}, bf16[8,16,256]{2,1,0:T(8,128)(2,1)S(1)}, u32[]{:S(2)}, u32[]{:S(2)}) collective-permute-start(bf16[8,16,256]{2,1,0:T(8,128)(2,1)S(1)} %get-tuple-element.33), channel_id=1, source_target_pairs={{0,2},{1,3},{2,0},{3,1},{4,6},{5,7},{6,4},{7,5},{8,10},{9,11},{10,... | collective-permute-start | bytes 196616 | tf_op jit(solution)/shard_map/ppermute | solution.py:470
  9.3 0.0 collective-permute-start.12
  9.3 1.8 %collective-permute-start.13 = (bf16[8,16,256]{2,1,0:T(8,128)(2,1)S(1)}, bf16[8,16,256]{2,1,0:T(8,128)(2,1)S(1)}, u32[]{:S(2)}, u32[]{:S(2)}) collective-permute-start(bf16[8,16,256]{2,1,0:T(8,128)(2,1)S(1)} %get-tuple-element.35), channel_id=1, source_target_pairs={{0,4},{1,5},{2,6},{3,7},{4,0},{5,1},{6,2},{7,3},{8,12},{9,13},{10,... | collective-permute-start | bytes 196616 | tf_op jit(solution)/shard_map/ppermute | solution.py:470
  11.1 0.0 collective-permute-start.14
  11.1 0.0 collective-permute-done.10.rest_1_
  11.1 2.6 %collective-permute-start.15 = (bf16[8,16,256]{2,1,0:T(8,128)(2,1)S(1)}, bf16[8,16,256]{2,1,0:T(8,128)(2,1)S(1)}, u32[]{:S(2)}, u32[]{:S(2)}) collective-permute-start(bf16[8,16,256]{2,1,0:T(8,128)(2,1)S(1)} %get-tuple-element.37), channel_id=1, source_target_pairs={{0,6},{1,7},{2,4},{3,5},{4,2},{5,3},{6,0},{7,1},{8,14},{9,15},{10,... | collective-permute-start | bytes 196616 | tf_op jit(solution)/shard_map/ppermute | solution.py:470
  13.7 0.0 collective-permute-done.11.rest_2_
  13.7 0.1 collective-permute-start.16
  13.8 1.7 %branch_next.1 = (bf16[8,16,256]{2,1,0:T(8,128)(2,1)S(1)}, bf16[8,16,256]{2,1,0:T(8,128)(2,1)S(1)}, bf16[8,16,256]{2,1,0:T(8,128)(2,1)S(1)}, bf16[8,16,256]{2,1,...) custom-call(s32[1]{0:T(128)} %bitcast.1.place_ref, ...), custom_call_target="tpu_custom_call" | custom-call | flops 402653184 | bytes 524288 | tf_op jit(solution)/shard_map/branch_next/pallas_call | solution.py:306
  15.5 0.0 collective-permute-done.12.rest_3_
  15.6 1.5 %collective-permute-start = (bf16[8,16,256]{2,1,0:T(8,128)(2,1)S(1)}, bf16[8,16,256]{2,1,0:T(8,128)(2,1)S(1)}, u32[]{:S(2)}, u32[]{:S(2)}) collective-permute-start(bf16[8,16,256]{2,1,0:T(8,128)(2,1)S(1)} %get-tuple-element.24), channel_id=1, source_target_pairs={{0,1},{1,0},{2,3},{3,2},{4,5},{5,4},{6,7},{7,6},{8,9},{9,8},{10,11... | collective-permute-start | bytes 196616 | tf_op jit(solution)/shard_map/ppermute | solution.py:470
  17.1 0.0 collective-permute-done.13.rest_4_
  17.1 0.5 collective-permute-start.1
  17.6 0.0 collective-permute-done.14.rest_5_
  17.6 1.6 %collective-permute-start.2 = (bf16[8,16,256]{2,1,0:T(8,128)(2,1)S(1)}, bf16[8,16,256]{2,1,0:T(8,128)(2,1)S(1)}, u32[]{:S(2)}, u32[]{:S(2)}) collective-permute-start(bf16[8,16,256]{2,1,0:T(8,128)(2,1)S(1)} %get-tuple-element.26), channel_id=1, source_target_pairs={{0,3},{1,2},{2,1},{3,0},{4,7},{5,6},{6,5},{7,4},{8,11},{9,10},{10,... | collective-permute-start | bytes 196616 | tf_op jit(solution)/shard_map/ppermute | solution.py:470
  19.2 0.0 collective-permute-done.15.rest_6_
  19.2 0.0 collective-permute-done.16.rest_7_
  19.2 0.9 %bands.3.right_ref.rest_1_ = bf16[4,128,256]{2,1,0:T(8,128)(2,1)S(1)} custom-call(s32[1]{0:T(128)} %bitcast.1.place_ref, bf16[8,16,256]{2,1,0:T(8,128)(2,1)S(1)} %get-tuple-element.31.rest_0_, bf16[8,16,256]{2,1,0:T(8,128)(2,1)S(1)} %collective-permute-done.10.rest_1_, bf16[8,16,256]{2,1,0:T(8,128)(2,1)S(1)} %collective-permute-done.11.rest_2_, ...), custom_call_target="tpu_custom_call" | custom-call | bytes 786432 | tf_op jit(solution)/shard_map/bands/pallas_call | solution.py:346
  20.1 1.6 %collective-permute-start.17 = (bf16[4,128,256]{2,1,0:T(8,128)(2,1)S(1)}, bf16[4,128,256]{2,1,0:T(8,128)(2,1)S(1)}, u32[]{:S(2)}, u32[]{:S(2)}) collective-permute-start(bf16[4,128,256]{2,1,0:T(8,128)(2,1)S(1)} %bands.3.right_ref.rest_1_), channel_id=1, source_target_pairs={{0,8},{8,16},{16,24},{24,0},{1,9},{9,17},{17,25},{25,1},{2,10},{10... | collective-permute-start | bytes 786440 | tf_op jit(solution)/shard_map/ppermute | solution.py:482
  21.8 1.6 %collective-permute-start.3 = (bf16[8,16,256]{2,1,0:T(8,128)(2,1)S(1)}, bf16[8,16,256]{2,1,0:T(8,128)(2,1)S(1)}, u32[]{:S(2)}, u32[]{:S(2)}) collective-permute-start(bf16[8,16,256]{2,1,0:T(8,128)(2,1)S(1)} %get-tuple-element.27), channel_id=1, source_target_pairs={{0,4},{1,5},{2,6},{3,7},{4,0},{5,1},{6,2},{7,3},{8,12},{9,13},{10,... | collective-permute-start | bytes 196616 | tf_op jit(solution)/shard_map/ppermute | solution.py:470
  23.3 0.0 collective-permute-done.rest_1_
  23.3 0.0 collective-permute-start.4
  23.3 0.0 collective-permute-done.1.rest_2_
  23.3 1.0 %collective-permute-start.5 = (bf16[8,16,256]{2,1,0:T(8,128)(2,1)S(1)}, bf16[8,16,256]{2,1,0:T(8,128)(2,1)S(1)}, u32[]{:S(2)}, u32[]{:S(2)}) collective-permute-start(bf16[8,16,256]{2,1,0:T(8,128)(2,1)S(1)} %get-tuple-element.29), channel_id=1, source_target_pairs={{0,6},{1,7},{2,4},{3,5},{4,2},{5,3},{6,0},{7,1},{8,14},{9,15},{10,... | collective-permute-start | bytes 196616 | tf_op jit(solution)/shard_map/ppermute | solution.py:470
  24.3 0.0 collective-permute-done.2.rest_3_
  24.3 1.8 %collective-permute-start.6 = (bf16[8,16,256]{2,1,0:T(8,128)(2,1)S(1)}, bf16[8,16,256]{2,1,0:T(8,128)(2,1)S(1)}, u32[]{:S(2)}, u32[]{:S(2)}) collective-permute-start(bf16[8,16,256]{2,1,0:T(8,128)(2,1)S(1)} %get-tuple-element.30), channel_id=1, source_target_pairs={{0,7},{1,6},{2,5},{3,4},{4,3},{5,2},{6,1},{7,0},{8,15},{9,14},{10,... | collective-permute-start | bytes 196616 | tf_op jit(solution)/shard_map/ppermute | solution.py:470
  26.2 0.0 collective-permute-done.3.rest_4_
  26.2 3.1 %collective-permute-done.4.rest_5_ = bf16[8,16,256]{2,1,0:T(8,128)(2,1)S(1)} collective-permute-done((bf16[8,16,256]{2,1,0:T(8,128)(2,1)S(1)}, bf16[8,16,256]{2,1,0:T(8,128)(2,1)S(1)}, u32[]{:S(2)}, u32[]{:S(2)}) %collective-permute-start.4) | collective-permute-done | bytes 65568 | tf_op jit(solution)/shard_map/ppermute | solution.py:470
  29.2 0.1 collective-permute-done.5.rest_6_
  29.3 0.5 collective-permute-done.6.rest_7_
  29.8 0.9 %bands.2.right_ref.rest_2_ = bf16[4,128,256]{2,1,0:T(8,128)(2,1)S(1)} custom-call(s32[1]{0:T(128)} %bitcast.1.place_ref, bf16[8,16,256]{2,1,0:T(8,128)(2,1)S(1)} %get-tuple-element.23.rest_0_, bf16[8,16,256]{2,1,0:T(8,128)(2,1)S(1)} %collective-permute-done.rest_1_, bf16[8,16,256]{2,1,0:T(8,128)(2,1)S(1)} %collective-permute-done.1.rest_2_, ...), custom_call_target="tpu_custom_call" | custom-call | bytes 786432 | tf_op jit(solution)/shard_map/bands/pallas_call | solution.py:346
  30.7 1.6 %collective-permute-start.7 = (bf16[4,128,256]{2,1,0:T(8,128)(2,1)S(1)}, bf16[4,128,256]{2,1,0:T(8,128)(2,1)S(1)}, u32[]{:S(2)}, u32[]{:S(2)}) collective-permute-start(bf16[4,128,256]{2,1,0:T(8,128)(2,1)S(1)} %bands.2.right_ref.rest_2_), channel_id=1, source_target_pairs={{0,8},{8,16},{16,24},{24,0},{1,9},{9,17},{17,25},{25,1},{2,10},{10... | collective-permute-start | bytes 786440 | tf_op jit(solution)/shard_map/ppermute | solution.py:482
  32.3 2.2 %collective-permute-start.19 = (bf16[4,128,256]{2,1,0:T(8,128)(2,1)S(1)}, bf16[4,128,256]{2,1,0:T(8,128)(2,1)S(1)}, u32[]{:S(2)}, u32[]{:S(2)}) collective-permute-start(bf16[4,128,256]{2,1,0:T(8,128)(2,1)S(1)} %bands.3.right_ref.rest_1_), channel_id=1, source_target_pairs={{0,24},{8,0},{16,8},{24,16},{1,25},{9,1},{17,9},{25,17},{2,26},{10... | collective-permute-start | bytes 786440 | tf_op jit(solution)/shard_map/ppermute | solution.py:483
  34.5 0.0 collective-permute-done.17.rest_3_
  34.5 0.0 collective-permute-start.18
  34.5 0.3 left.3.rest_0_
  34.9 3.9 %collective-permute-start.9 = (bf16[4,128,256]{2,1,0:T(8,128)(2,1)S(1)}, bf16[4,128,256]{2,1,0:T(8,128)(2,1)S(1)}, u32[]{:S(2)}, u32[]{:S(2)}) collective-permute-start(bf16[4,128,256]{2,1,0:T(8,128)(2,1)S(1)} %bands.2.right_ref.rest_2_), channel_id=1, source_target_pairs={{0,24},{8,0},{16,8},{24,16},{1,25},{9,1},{17,9},{25,17},{2,26},{10... | collective-permute-start | bytes 786440 | tf_op jit(solution)/shard_map/ppermute | solution.py:483
  38.8 3.6 %correlate.5.rest_5_ = f32[4,8,2,256,1024]{4,3,2,1,0:T(8,128)} custom-call(s32[1]{0:T(128)} %bitcast.me_ref, bf16[2,4,256,128]{3,2,1,0:T(8,128)(2,1)S(1)} %left.3.rest_0_, bf16[4,128,256]{2,1,0:T(8,128)(2,1)S(1)} %bands.3.right_ref.rest_1_), custom_call_target="tpu_custom_call" | custom-call | flops 536870912 | bytes 8388608 | tf_op jit(solution)/shard_map/correlate/pallas_call | solution.py:432
  42.4 0.3 left.2.rest_1_.rest_0_
  42.7 0.0 collective-permute-done.7.rest_3_
  42.7 3.0 %collective-permute-start.8 = (bf16[4,128,256]{2,1,0:T(8,128)(2,1)S(1)}, bf16[4,128,256]{2,1,0:T(8,128)(2,1)S(1)}, u32[]{:S(2)}, u32[]{:S(2)}) collective-permute-start(bf16[4,128,256]{2,1,0:T(8,128)(2,1)S(1)} %collective-permute-done.7.rest_3_), channel_id=1, source_target_pairs={{0,8},{8,16},{16,24},{24,0},{1,9},{9,17},{17,25},{25,1},{2,10},{10... | collective-permute-start | bytes 786440 | tf_op jit(solution)/shard_map/ppermute | solution.py:484
  45.7 1.7 %collective-permute-done.19.rest_4_ = bf16[4,128,256]{2,1,0:T(8,128)(2,1)S(1)} collective-permute-done((bf16[4,128,256]{2,1,0:T(8,128)(2,1)S(1)}, bf16[4,128,256]{2,1,0:T(8,128)(2,1)S(1)}, u32[]{:S(2)}, u32[]{:S(2)}) %collective-permute-start.19) | collective-permute-done | bytes 262176 | tf_op jit(solution)/shard_map/ppermute | solution.py:483
  47.4 8.7 %correlate.6.rest_4_ = f32[4,8,2,256,1024]{4,3,2,1,0:T(8,128)} custom-call(s32[1]{0:T(128)} %bitcast.me_ref, bf16[2,4,256,128]{3,2,1,0:T(8,128)(2,1)S(1)} %left.3.rest_0_, bf16[2,4,256,128]{3,2,1,0:T(8,128)(2,1)S(1)} %left.2.rest_1_.rest_0_, bf16[4,128,256]{2,1,0:T(8,128)(2,1)S(1)} %bands.2.right_ref.rest_2_, ...), custom_call_target="tpu_custom_call", output_to_operand_aliasing={{}: (6, {})} | custom-call | flops 1610612736 | bytes 25165824 | tf_op jit(solution)/shard_map/correlate/pallas_call | solution.py:432
  56.1 0.0 collective-permute-done.18.rest_2_
  56.1 6.2 %correlate.7.rest_2_ = f32[4,8,2,256,1024]{4,3,2,1,0:T(8,128)} custom-call(s32[1]{0:T(128)} %bitcast.me_ref, bf16[2,4,256,128]{3,2,1,0:T(8,128)(2,1)S(1)} %left.3.rest_0_, bf16[2,4,256,128]{3,2,1,0:T(8,128)(2,1)S(1)} %left.2.rest_1_.rest_0_, bf16[4,128,256]{2,1,0:T(8,128)(2,1)S(1)} %collective-permute-done.18.rest_2_, ...), custom_call_target="tpu_custom_call", output_to_operand_aliasing={{}: (5, {})} | custom-call | flops 1073741824 | bytes 16777216 | tf_op jit(solution)/shard_map/correlate/pallas_call | solution.py:432
  62.3 0.0 collective-permute-done.9.rest_1_
  62.3 3.6 %correlate.8.rest_2_ = f32[4,8,2,256,1024]{4,3,2,1,0:T(8,128)} custom-call(s32[1]{0:T(128)} %bitcast.me_ref, bf16[2,4,256,128]{3,2,1,0:T(8,128)(2,1)S(1)} %left.2.rest_1_.rest_0_, bf16[4,128,256]{2,1,0:T(8,128)(2,1)S(1)} %collective-permute-done.9.rest_1_, f32[4,8,2,256,1024]{4,3,2,1,0:T(8,128)} %correlate.7.rest_2_), custom_call_target="tpu_custom_call", output_to_operand_aliasing={{}: (3, {})} | custom-call | flops 536870912 | bytes 8388608 | tf_op jit(solution)/shard_map/correlate/pallas_call | solution.py:432
  65.9 0.0 collective-permute-done.8.rest_1_
  65.9 3.6 %correlate.9 = f32[4,8,2,256,1024]{4,3,2,1,0:T(8,128)} custom-call(s32[1]{0:T(128)} %bitcast.me_ref, bf16[2,4,256,128]{3,2,1,0:T(8,128)(2,1)S(1)} %left.2.rest_1_.rest_0_, bf16[4,128,256]{2,1,0:T(8,128)(2,1)S(1)} %collective-permute-done.8.rest_1_, f32[4,8,2,256,1024]{4,3,2,1,0:T(8,128)} %correlate.8.rest_2_), custom_call_target="tpu_custom_call", output_to_operand_aliasing={{}: (3, {})} | custom-call | flops 536870912 | bytes 8388608 | tf_op jit(solution)/shard_map/correlate/pallas_call | solution.py:432
Async XLA Ops:
  6.2 4.9 %collective-permute-start.10 = (bf16[8,16,256]{2,1,0:T(8,128)(2,1)S(1)}, bf16[8,16,256]{2,1,0:T(8,128)(2,1)S(1)}, u32[]{:S(2)}, u32[]{:S(2)}) collective-permute-start(bf16[8,16,256]{2,1,0:T(8,128)(2,1)S(1)} %get-tuple-element.32), channel_id=1, source_target_pairs={{0,1},{1,0},{2,3},{3,2},{4,5},{5,4},{6,7},{7,6},{8,9},{9,8},{10,11... | collective-permute-start | bytes 196616 | tf_op jit(solution)/shard_map/ppermute | solution.py:470
  6.7 7.0 %collective-permute-start.11 = (bf16[8,16,256]{2,1,0:T(8,128)(2,1)S(1)}, bf16[8,16,256]{2,1,0:T(8,128)(2,1)S(1)}, u32[]{:S(2)}, u32[]{:S(2)}) collective-permute-start(bf16[8,16,256]{2,1,0:T(8,128)(2,1)S(1)} %get-tuple-element.33), channel_id=1, source_target_pairs={{0,2},{1,3},{2,0},{3,1},{4,6},{5,7},{6,4},{7,5},{8,10},{9,11},{10,... | collective-permute-start | bytes 196616 | tf_op jit(solution)/shard_map/ppermute | solution.py:470
  9.3 6.3 %collective-permute-start.12 = (bf16[8,16,256]{2,1,0:T(8,128)(2,1)S(1)}, bf16[8,16,256]{2,1,0:T(8,128)(2,1)S(1)}, u32[]{:S(2)}, u32[]{:S(2)}) collective-permute-start(bf16[8,16,256]{2,1,0:T(8,128)(2,1)S(1)} %get-tuple-element.34), channel_id=1, source_target_pairs={{0,3},{1,2},{2,1},{3,0},{4,7},{5,6},{6,5},{7,4},{8,11},{9,10},{10,... | collective-permute-start | bytes 196616 | tf_op jit(solution)/shard_map/ppermute | solution.py:470
  9.3 7.8 %collective-permute-start.13 = (bf16[8,16,256]{2,1,0:T(8,128)(2,1)S(1)}, bf16[8,16,256]{2,1,0:T(8,128)(2,1)S(1)}, u32[]{:S(2)}, u32[]{:S(2)}) collective-permute-start(bf16[8,16,256]{2,1,0:T(8,128)(2,1)S(1)} %get-tuple-element.35), channel_id=1, source_target_pairs={{0,4},{1,5},{2,6},{3,7},{4,0},{5,1},{6,2},{7,3},{8,12},{9,13},{10,... | collective-permute-start | bytes 196616 | tf_op jit(solution)/shard_map/ppermute | solution.py:470
  11.1 6.5 %collective-permute-start.14 = (bf16[8,16,256]{2,1,0:T(8,128)(2,1)S(1)}, bf16[8,16,256]{2,1,0:T(8,128)(2,1)S(1)}, u32[]{:S(2)}, u32[]{:S(2)}) collective-permute-start(bf16[8,16,256]{2,1,0:T(8,128)(2,1)S(1)} %get-tuple-element.36), channel_id=1, source_target_pairs={{0,5},{1,4},{2,7},{3,6},{4,1},{5,0},{6,3},{7,2},{8,13},{9,12},{10,... | collective-permute-start | bytes 196616 | tf_op jit(solution)/shard_map/ppermute | solution.py:470
  11.1 8.1 %collective-permute-start.15 = (bf16[8,16,256]{2,1,0:T(8,128)(2,1)S(1)}, bf16[8,16,256]{2,1,0:T(8,128)(2,1)S(1)}, u32[]{:S(2)}, u32[]{:S(2)}) collective-permute-start(bf16[8,16,256]{2,1,0:T(8,128)(2,1)S(1)} %get-tuple-element.37), channel_id=1, source_target_pairs={{0,6},{1,7},{2,4},{3,5},{4,2},{5,3},{6,0},{7,1},{8,14},{9,15},{10,... | collective-permute-start | bytes 196616 | tf_op jit(solution)/shard_map/ppermute | solution.py:470
  13.7 5.5 %collective-permute-start.16 = (bf16[8,16,256]{2,1,0:T(8,128)(2,1)S(1)}, bf16[8,16,256]{2,1,0:T(8,128)(2,1)S(1)}, u32[]{:S(2)}, u32[]{:S(2)}) collective-permute-start(bf16[8,16,256]{2,1,0:T(8,128)(2,1)S(1)} %get-tuple-element.38), channel_id=1, source_target_pairs={{0,7},{1,6},{2,5},{3,4},{4,3},{5,2},{6,1},{7,0},{8,15},{9,14},{10,... | collective-permute-start | bytes 196616 | tf_op jit(solution)/shard_map/ppermute | solution.py:470
  15.6 7.8 %collective-permute-start = (bf16[8,16,256]{2,1,0:T(8,128)(2,1)S(1)}, bf16[8,16,256]{2,1,0:T(8,128)(2,1)S(1)}, u32[]{:S(2)}, u32[]{:S(2)}) collective-permute-start(bf16[8,16,256]{2,1,0:T(8,128)(2,1)S(1)} %get-tuple-element.24), channel_id=1, source_target_pairs={{0,1},{1,0},{2,3},{3,2},{4,5},{5,4},{6,7},{7,6},{8,9},{9,8},{10,11... | collective-permute-start | bytes 196616 | tf_op jit(solution)/shard_map/ppermute | solution.py:470
  17.1 6.2 %collective-permute-start.1 = (bf16[8,16,256]{2,1,0:T(8,128)(2,1)S(1)}, bf16[8,16,256]{2,1,0:T(8,128)(2,1)S(1)}, u32[]{:S(2)}, u32[]{:S(2)}) collective-permute-start(bf16[8,16,256]{2,1,0:T(8,128)(2,1)S(1)} %get-tuple-element.25), channel_id=1, source_target_pairs={{0,2},{1,3},{2,0},{3,1},{4,6},{5,7},{6,4},{7,5},{8,10},{9,11},{10,... | collective-permute-start | bytes 196616 | tf_op jit(solution)/shard_map/ppermute | solution.py:470
  17.6 6.7 %collective-permute-start.2 = (bf16[8,16,256]{2,1,0:T(8,128)(2,1)S(1)}, bf16[8,16,256]{2,1,0:T(8,128)(2,1)S(1)}, u32[]{:S(2)}, u32[]{:S(2)}) collective-permute-start(bf16[8,16,256]{2,1,0:T(8,128)(2,1)S(1)} %get-tuple-element.26), channel_id=1, source_target_pairs={{0,3},{1,2},{2,1},{3,0},{4,7},{5,6},{6,5},{7,4},{8,11},{9,10},{10,... | collective-permute-start | bytes 196616 | tf_op jit(solution)/shard_map/ppermute | solution.py:470
  20.1 14.4 %collective-permute-start.17 = (bf16[4,128,256]{2,1,0:T(8,128)(2,1)S(1)}, bf16[4,128,256]{2,1,0:T(8,128)(2,1)S(1)}, u32[]{:S(2)}, u32[]{:S(2)}) collective-permute-start(bf16[4,128,256]{2,1,0:T(8,128)(2,1)S(1)} %bands.3.right_ref.rest_1_), channel_id=1, source_target_pairs={{0,8},{8,16},{16,24},{24,0},{1,9},{9,17},{17,25},{25,1},{2,10},{10... | collective-permute-start | bytes 786440 | tf_op jit(solution)/shard_map/ppermute | solution.py:482
  21.8 4.4 %collective-permute-start.3 = (bf16[8,16,256]{2,1,0:T(8,128)(2,1)S(1)}, bf16[8,16,256]{2,1,0:T(8,128)(2,1)S(1)}, u32[]{:S(2)}, u32[]{:S(2)}) collective-permute-start(bf16[8,16,256]{2,1,0:T(8,128)(2,1)S(1)} %get-tuple-element.27), channel_id=1, source_target_pairs={{0,4},{1,5},{2,6},{3,7},{4,0},{5,1},{6,2},{7,3},{8,12},{9,13},{10,... | collective-permute-start | bytes 196616 | tf_op jit(solution)/shard_map/ppermute | solution.py:470
  23.3 5.9 %collective-permute-start.4 = (bf16[8,16,256]{2,1,0:T(8,128)(2,1)S(1)}, bf16[8,16,256]{2,1,0:T(8,128)(2,1)S(1)}, u32[]{:S(2)}, u32[]{:S(2)}) collective-permute-start(bf16[8,16,256]{2,1,0:T(8,128)(2,1)S(1)} %get-tuple-element.28), channel_id=1, source_target_pairs={{0,5},{1,4},{2,7},{3,6},{4,1},{5,0},{6,3},{7,2},{8,13},{9,12},{10,... | collective-permute-start | bytes 196616 | tf_op jit(solution)/shard_map/ppermute | solution.py:470
  23.3 6.0 %collective-permute-start.5 = (bf16[8,16,256]{2,1,0:T(8,128)(2,1)S(1)}, bf16[8,16,256]{2,1,0:T(8,128)(2,1)S(1)}, u32[]{:S(2)}, u32[]{:S(2)}) collective-permute-start(bf16[8,16,256]{2,1,0:T(8,128)(2,1)S(1)} %get-tuple-element.29), channel_id=1, source_target_pairs={{0,6},{1,7},{2,4},{3,5},{4,2},{5,3},{6,0},{7,1},{8,14},{9,15},{10,... | collective-permute-start | bytes 196616 | tf_op jit(solution)/shard_map/ppermute | solution.py:470
  24.3 5.4 %collective-permute-start.6 = (bf16[8,16,256]{2,1,0:T(8,128)(2,1)S(1)}, bf16[8,16,256]{2,1,0:T(8,128)(2,1)S(1)}, u32[]{:S(2)}, u32[]{:S(2)}) collective-permute-start(bf16[8,16,256]{2,1,0:T(8,128)(2,1)S(1)} %get-tuple-element.30), channel_id=1, source_target_pairs={{0,7},{1,6},{2,5},{3,4},{4,3},{5,2},{6,1},{7,0},{8,15},{9,14},{10,... | collective-permute-start | bytes 196616 | tf_op jit(solution)/shard_map/ppermute | solution.py:470
  30.7 12.1 %collective-permute-start.7 = (bf16[4,128,256]{2,1,0:T(8,128)(2,1)S(1)}, bf16[4,128,256]{2,1,0:T(8,128)(2,1)S(1)}, u32[]{:S(2)}, u32[]{:S(2)}) collective-permute-start(bf16[4,128,256]{2,1,0:T(8,128)(2,1)S(1)} %bands.2.right_ref.rest_2_), channel_id=1, source_target_pairs={{0,8},{8,16},{16,24},{24,0},{1,9},{9,17},{17,25},{25,1},{2,10},{10... | collective-permute-start | bytes 786440 | tf_op jit(solution)/shard_map/ppermute | solution.py:482
  32.3 15.1 %collective-permute-start.19 = (bf16[4,128,256]{2,1,0:T(8,128)(2,1)S(1)}, bf16[4,128,256]{2,1,0:T(8,128)(2,1)S(1)}, u32[]{:S(2)}, u32[]{:S(2)}) collective-permute-start(bf16[4,128,256]{2,1,0:T(8,128)(2,1)S(1)} %bands.3.right_ref.rest_1_), channel_id=1, source_target_pairs={{0,24},{8,0},{16,8},{24,16},{1,25},{9,1},{17,9},{25,17},{2,26},{10... | collective-permute-start | bytes 786440 | tf_op jit(solution)/shard_map/ppermute | solution.py:483
  34.5 21.5 %collective-permute-start.18 = (bf16[4,128,256]{2,1,0:T(8,128)(2,1)S(1)}, bf16[4,128,256]{2,1,0:T(8,128)(2,1)S(1)}, u32[]{:S(2)}, u32[]{:S(2)}) collective-permute-start(bf16[4,128,256]{2,1,0:T(8,128)(2,1)S(1)} %collective-permute-done.17.rest_3_), channel_id=1, source_target_pairs={{0,8},{8,16},{16,24},{24,0},{1,9},{9,17},{17,25},{25,1},{2,10},{10... | collective-permute-start | bytes 786440 | tf_op jit(solution)/shard_map/ppermute | solution.py:484
  34.9 27.4 %collective-permute-start.9 = (bf16[4,128,256]{2,1,0:T(8,128)(2,1)S(1)}, bf16[4,128,256]{2,1,0:T(8,128)(2,1)S(1)}, u32[]{:S(2)}, u32[]{:S(2)}) collective-permute-start(bf16[4,128,256]{2,1,0:T(8,128)(2,1)S(1)} %bands.2.right_ref.rest_2_), channel_id=1, source_target_pairs={{0,24},{8,0},{16,8},{24,16},{1,25},{9,1},{17,9},{25,17},{2,26},{10... | collective-permute-start | bytes 786440 | tf_op jit(solution)/shard_map/ppermute | solution.py:483
  42.7 23.2 %collective-permute-start.8 = (bf16[4,128,256]{2,1,0:T(8,128)(2,1)S(1)}, bf16[4,128,256]{2,1,0:T(8,128)(2,1)S(1)}, u32[]{:S(2)}, u32[]{:S(2)}) collective-permute-start(bf16[4,128,256]{2,1,0:T(8,128)(2,1)S(1)} %collective-permute-done.7.rest_3_), channel_id=1, source_target_pairs={{0,8},{8,16},{16,24},{24,0},{1,9},{9,17},{17,25},{25,1},{2,10},{10... | collective-permute-start | bytes 786440 | tf_op jit(solution)/shard_map/ppermute | solution.py:484

commit v3 on v2

--- a/solution.py
+++ b/solution.py
@@ -216,7 +216,7 @@
 
 def first_kernel(radix, dests, place_ref, volt_ref, taps_ref, far_ref, row_ref, low_ref, *rest):
     outs = rest[:dests]
-    y, volts, filtered, table, taps, far, row, low, volt_sems, sems = rest[dests:]
+    y, volts, products, filtered, table, taps, far, row, low, volt_sems, sems = rest[dests:]
     me = place_ref[0]
     parts, rows = volts.shape[0], volts.shape[1]
     small = table_copies(0, me, far_ref, row_ref, low_ref, far, row, low, sems)
@@ -234,7 +234,13 @@
     together = LANES // rows
     for i, load in enumerate(loads):
         load.wait()
-        filtered[pl.ds(i * rows, rows)] = jnp.sum(volts[i].astype(jnp.float32) * by_frame[None], axis=1)
+        frames = volts.shape[2]
+        product = volts[i].astype(jnp.float32) * by_frame[None]
+        for a in range(radix):
+            columns = slice(a * LANES, (a + 1) * LANES)
+            products[i % 2, a] = product[:, :, columns].reshape(rows * frames, LANES)
+            terms = [products[i % 2, a, pl.ds(f, rows, stride=frames)] for f in range(frames)]
+            filtered[pl.ds(i * rows, rows), columns] = sum(terms)
         if (i + 1) % together:
             continue
         inputs = pl.ds((i + 1) * rows - LANES, LANES)
@@ -290,6 +296,7 @@
         out_specs=[near] * (dests + 1),
         scratch_shapes=[
             pltpu.VMEM((parts, inputs // parts, frames, slots), jnp.bfloat16),
+            pltpu.VMEM((2, radix, inputs // parts * frames, LANES), jnp.float32),
             pltpu.VMEM((inputs, slots), jnp.float32),
             table,
             pltpu.VMEM((tap_count, slots), jnp.float32),
@@ -316,25 +323,36 @@
     return [[near_memory(x) for x in part] for part in result]
 
 
+def swapped(flag, low, high):
+    return jnp.where(flag, high, low), jnp.where(flag, low, high)
+
+
+def in_order(pieces, me, bit=0):
+    step = 1 << bit
+    if step == len(pieces):
+        return pieces
+    pieces = list(pieces)
+    flag = lax.bitwise_and(me, step) != 0
+    for k in range(len(pieces)):
+        if not k & step:
+            pieces[k], pieces[k + step] = swapped(flag, pieces[k], pieces[k + step])
+    return in_order(pieces, me, bit + 1)
+
+
 def band_kernel(place_ref, *rest):
-    out_ref, turned, sems = rest[-3:]
-    phases, radix, rows, _ = turned.shape
-    blocks = rest[:phases]
+    blocks, out_ref = rest[:-1], rest[-1]
+    phases = len(blocks)
+    radix, rows, _ = blocks[0].shape
+    near, half = rows // 2, phases // 2
     me = place_ref[0]
-    loads = [
-        pltpu.make_async_copy(blocks[k], turned.at[lax.bitwise_xor(me, k)], sems.at[k]) for k in range(phases)
-    ]
-    for load in loads:
-        load.start()
-    for load in loads:
-        load.wait()
-    near = rows // 2
+    sign = jnp.where(lax.bitwise_and(me, half) != 0, -1.0, 1.0).astype(jnp.float32)
     for u in range(radix):
-        pair = [turned[p, u].astype(jnp.float32) for p in range(phases)]
-        re_pair, im_pair = half_sums([x[:near] for x in pair]), half_sums([x[near:] for x in pair])
-        for c in range(phases // 2):
-            cos_w, sin_w = turn_weights(phases // 2, c, phases)
-            terms = re_pair[c % 2] + im_pair[c % 2]
+        full = [block[u].astype(jnp.float32) for block in blocks]
+        sums, differences = half_sums(full)
+        pair = [in_order(sums, me), in_order([d * sign for d in differences], me)]
+        for c in range(half):
+            cos_w, sin_w = turn_weights(half, c, phases)
+            terms = [x[:near] for x in pair[c % 2]] + [x[near:] for x in pair[c % 2]]
             spectrum = [weighted(terms, cos_w + [-w for w in sin_w]), weighted(terms, sin_w + cos_w)]
             out_ref[c, u * rows : (u + 1) * rows] = jnp.concatenate(spectrum, axis=0).astype(jnp.bfloat16)
 
@@ -348,10 +366,6 @@
         out_shape=pltpu.VMEM((bands, depth, inputs), jnp.bfloat16),
         in_specs=[pl.BlockSpec(memory_space=pltpu.SMEM)] + [pl.BlockSpec(memory_space=pltpu.VMEM)] * phases,
         out_specs=pl.BlockSpec(memory_space=pltpu.VMEM),
-        scratch_shapes=[
-            pltpu.VMEM((phases, radix, rows, inputs), jnp.bfloat16),
-            pltpu.SemaphoreType.DMA((phases,)),
-        ],
         cost_estimate=pl.CostEstimate(flops=0, transcendentals=0, bytes_accessed=6 * bands * depth * inputs),
         name="bands",
     )(me.reshape(1), *blocks)

time: 69.7 us -> 67.7 us (0.971)
  Pallas kernels: 36 us -> 34 us
    pallas_call x2, Pallas kernels: 1.8 us -> 0.49 us  [bands_of(): pl.pallas_call(band_kernel, out_shape=pltpu.VMEM((bands, depth, inputs),...]
  transfers between devices with their start and end apart: 20 -> 20, of which waited for: 4 -> 4; matrix products, arithmetic and copies ran while one was open for 0% -> 0% of each run, Pallas kernels for 38% -> 37%
where the time goes in v3:
time: 67.7 us; the launch traced here: 67.5 us
  Pallas kernels  34 us (50%)
  starting transfers between devices  28.1 us (42%)
  waiting for transfers between devices  5.31 us (8%)
    pallas_call x5, Pallas kernels, correlate(): pl.pallas_call(functools.partial(correlate_kernel, near, group, listed, s...  25.7 us
    ppermute x14, starting transfers between devices, one_frame(): blocks[k] = near_memory(lax.ppermute(blocks[k], 'chan', route))  15.7 us
    ppermute x2, starting transfers between devices, one_frame(): last.append(near_memory(lax.ppermute(x, 'stn', backward)))  6.12 us
    pallas_call x1, Pallas kernels, branch_of(): pl.pallas_call(functools.partial(first_kernel, radix, dests), out_shape=b...  5.46 us
    ppermute x14, waiting for transfers between devices, one_frame(): blocks[k] = near_memory(lax.ppermute(blocks[k], 'chan', route))  3.63 us
    ppermute x2, starting transfers between devices, one_frame(): first.append(near_memory(lax.ppermute(x, 'stn', onward)))  3.26 us
    ppermute x2, starting transfers between devices, one_frame(): second.append(near_memory(lax.ppermute(first[h], 'stn', onward)))  3.01 us
    pallas_call x1, Pallas kernels, branch_of(): pl.pallas_call(functools.partial(next_kernel, half, dests), out_shape=blo...  1.69 us
  transfers between devices with their start and end apart: 20, of which 4 were waited for; matrix products, arithmetic and copies ran while one was open for 0% of the time, Pallas kernels for 37%

profile of v3, /device:TPU:0, one launch (start us, length us, event | category | flops | bytes accessed | tf_op | source)
XLA Modules:
  0.0 67.5 jit_solution(1906604904782599425)
XLA Ops:
  0.0 5.5 %branch.1 = (bf16[8,16,256]{2,1,0:T(8,128)(2,1)S(1)}, bf16[8,16,256]{2,1,0:T(8,128)(2,1)S(1)}, bf16[8,16,256]{2,1,0:T(8,128)(2,1)S(1)}, bf16[8,16,256]{2,1,0:T(8...) custom-call(s32[1]{0:T(128)} %bitcast.1.place_ref, ...), custom_call_target="tpu_custom_call" | custom-call | flops 402653184 | bytes 4194304 | tf_op jit(solution)/shard_map/branch/pallas_call | solution.py:292
  5.5 0.6 collective-permute-start.10
  6.0 2.5 %collective-permute-start.11 = (bf16[8,16,256]{2,1,0:T(8,128)(2,1)S(1)}, bf16[8,16,256]{2,1,0:T(8,128)(2,1)S(1)}, u32[]{:S(2)}, u32[]{:S(2)}) collective-permute-start(bf16[8,16,256]{2,1,0:T(8,128)(2,1)S(1)} %get-tuple-element.33), channel_id=1, source_target_pairs={{0,2},{1,3},{2,0},{3,1},{4,6},{5,7},{6,4},{7,5},{8,10},{9,11},{10,... | collective-permute-start | bytes 196616 | tf_op jit(solution)/shard_map/ppermute | solution.py:484
  8.6 0.0 collective-permute-start.12
  8.6 1.8 %collective-permute-start.13 = (bf16[8,16,256]{2,1,0:T(8,128)(2,1)S(1)}, bf16[8,16,256]{2,1,0:T(8,128)(2,1)S(1)}, u32[]{:S(2)}, u32[]{:S(2)}) collective-permute-start(bf16[8,16,256]{2,1,0:T(8,128)(2,1)S(1)} %get-tuple-element.35), channel_id=1, source_target_pairs={{0,4},{1,5},{2,6},{3,7},{4,0},{5,1},{6,2},{7,3},{8,12},{9,13},{10,... | collective-permute-start | bytes 196616 | tf_op jit(solution)/shard_map/ppermute | solution.py:484
  10.4 0.0 collective-permute-start.14
  10.4 0.0 collective-permute-done.10.rest_1_
  10.4 2.6 %collective-permute-start.15 = (bf16[8,16,256]{2,1,0:T(8,128)(2,1)S(1)}, bf16[8,16,256]{2,1,0:T(8,128)(2,1)S(1)}, u32[]{:S(2)}, u32[]{:S(2)}) collective-permute-start(bf16[8,16,256]{2,1,0:T(8,128)(2,1)S(1)} %get-tuple-element.37), channel_id=1, source_target_pairs={{0,6},{1,7},{2,4},{3,5},{4,2},{5,3},{6,0},{7,1},{8,14},{9,15},{10,... | collective-permute-start | bytes 196616 | tf_op jit(solution)/shard_map/ppermute | solution.py:484
  13.0 0.0 collective-permute-done.11.rest_2_
  13.0 0.1 collective-permute-start.16
  13.1 1.7 %branch_next.1 = (bf16[8,16,256]{2,1,0:T(8,128)(2,1)S(1)}, bf16[8,16,256]{2,1,0:T(8,128)(2,1)S(1)}, bf16[8,16,256]{2,1,0:T(8,128)(2,1)S(1)}, bf16[8,16,256]{2,1,...) custom-call(s32[1]{0:T(128)} %bitcast.1.place_ref, ...), custom_call_target="tpu_custom_call" | custom-call | flops 402653184 | bytes 524288 | tf_op jit(solution)/shard_map/branch_next/pallas_call | solution.py:313
  14.8 0.0 collective-permute-done.12.rest_3_
  14.9 1.5 %collective-permute-start = (bf16[8,16,256]{2,1,0:T(8,128)(2,1)S(1)}, bf16[8,16,256]{2,1,0:T(8,128)(2,1)S(1)}, u32[]{:S(2)}, u32[]{:S(2)}) collective-permute-start(bf16[8,16,256]{2,1,0:T(8,128)(2,1)S(1)} %get-tuple-element.24), channel_id=1, source_target_pairs={{0,1},{1,0},{2,3},{3,2},{4,5},{5,4},{6,7},{7,6},{8,9},{9,8},{10,11... | collective-permute-start | bytes 196616 | tf_op jit(solution)/shard_map/ppermute | solution.py:484
  16.4 0.0 collective-permute-done.13.rest_4_
  16.4 0.5 collective-permute-start.1
  16.9 0.0 collective-permute-done.14.rest_5_
  16.9 1.6 %collective-permute-start.2 = (bf16[8,16,256]{2,1,0:T(8,128)(2,1)S(1)}, bf16[8,16,256]{2,1,0:T(8,128)(2,1)S(1)}, u32[]{:S(2)}, u32[]{:S(2)}) collective-permute-start(bf16[8,16,256]{2,1,0:T(8,128)(2,1)S(1)} %get-tuple-element.26), channel_id=1, source_target_pairs={{0,3},{1,2},{2,1},{3,0},{4,7},{5,6},{6,5},{7,4},{8,11},{9,10},{10,... | collective-permute-start | bytes 196616 | tf_op jit(solution)/shard_map/ppermute | solution.py:484
  18.5 0.0 collective-permute-done.15.rest_6_
  18.5 0.0 collective-permute-done.16.rest_7_
  18.5 0.2 bands.3.right_ref.rest_1_
  18.8 1.6 %collective-permute-start.17 = (bf16[4,128,256]{2,1,0:T(8,128)(2,1)S(1)}, bf16[4,128,256]{2,1,0:T(8,128)(2,1)S(1)}, u32[]{:S(2)}, u32[]{:S(2)}) collective-permute-start(bf16[4,128,256]{2,1,0:T(8,128)(2,1)S(1)} %bands.3.right_ref.rest_1_), channel_id=1, source_target_pairs={{0,8},{8,16},{16,24},{24,0},{1,9},{9,17},{17,25},{25,1},{2,10},{10... | collective-permute-start | bytes 786440 | tf_op jit(solution)/shard_map/ppermute | solution.py:496
  20.4 1.6 %collective-permute-start.3 = (bf16[8,16,256]{2,1,0:T(8,128)(2,1)S(1)}, bf16[8,16,256]{2,1,0:T(8,128)(2,1)S(1)}, u32[]{:S(2)}, u32[]{:S(2)}) collective-permute-start(bf16[8,16,256]{2,1,0:T(8,128)(2,1)S(1)} %get-tuple-element.27), channel_id=1, source_target_pairs={{0,4},{1,5},{2,6},{3,7},{4,0},{5,1},{6,2},{7,3},{8,12},{9,13},{10,... | collective-permute-start | bytes 196616 | tf_op jit(solution)/shard_map/ppermute | solution.py:484
  22.0 0.0 collective-permute-done.rest_1_
  22.0 0.0 collective-permute-start.4
  22.0 0.0 collective-permute-done.1.rest_2_
  22.0 1.0 %collective-permute-start.5 = (bf16[8,16,256]{2,1,0:T(8,128)(2,1)S(1)}, bf16[8,16,256]{2,1,0:T(8,128)(2,1)S(1)}, u32[]{:S(2)}, u32[]{:S(2)}) collective-permute-start(bf16[8,16,256]{2,1,0:T(8,128)(2,1)S(1)} %get-tuple-element.29), channel_id=1, source_target_pairs={{0,6},{1,7},{2,4},{3,5},{4,2},{5,3},{6,0},{7,1},{8,14},{9,15},{10,... | collective-permute-start | bytes 196616 | tf_op jit(solution)/shard_map/ppermute | solution.py:484
  23.0 0.0 collective-permute-done.2.rest_3_
  23.0 1.8 %collective-permute-start.6 = (bf16[8,16,256]{2,1,0:T(8,128)(2,1)S(1)}, bf16[8,16,256]{2,1,0:T(8,128)(2,1)S(1)}, u32[]{:S(2)}, u32[]{:S(2)}) collective-permute-start(bf16[8,16,256]{2,1,0:T(8,128)(2,1)S(1)} %get-tuple-element.30), channel_id=1, source_target_pairs={{0,7},{1,6},{2,5},{3,4},{4,3},{5,2},{6,1},{7,0},{8,15},{9,14},{10,... | collective-permute-start | bytes 196616 | tf_op jit(solution)/shard_map/ppermute | solution.py:484
  24.8 0.0 collective-permute-done.3.rest_4_
  24.8 3.1 %collective-permute-done.4.rest_5_ = bf16[8,16,256]{2,1,0:T(8,128)(2,1)S(1)} collective-permute-done((bf16[8,16,256]{2,1,0:T(8,128)(2,1)S(1)}, bf16[8,16,256]{2,1,0:T(8,128)(2,1)S(1)}, u32[]{:S(2)}, u32[]{:S(2)}) %collective-permute-start.4) | collective-permute-done | bytes 65568 | tf_op jit(solution)/shard_map/ppermute | solution.py:484
  27.9 0.1 collective-permute-done.5.rest_6_
  27.9 0.5 collective-permute-done.6.rest_7_
  28.4 0.2 bands.2.right_ref.rest_2_
  28.7 1.6 %collective-permute-start.7 = (bf16[4,128,256]{2,1,0:T(8,128)(2,1)S(1)}, bf16[4,128,256]{2,1,0:T(8,128)(2,1)S(1)}, u32[]{:S(2)}, u32[]{:S(2)}) collective-permute-start(bf16[4,128,256]{2,1,0:T(8,128)(2,1)S(1)} %bands.2.right_ref.rest_2_), channel_id=1, source_target_pairs={{0,8},{8,16},{16,24},{24,0},{1,9},{9,17},{17,25},{25,1},{2,10},{10... | collective-permute-start | bytes 786440 | tf_op jit(solution)/shard_map/ppermute | solution.py:496
  30.3 2.3 %collective-permute-start.19 = (bf16[4,128,256]{2,1,0:T(8,128)(2,1)S(1)}, bf16[4,128,256]{2,1,0:T(8,128)(2,1)S(1)}, u32[]{:S(2)}, u32[]{:S(2)}) collective-permute-start(bf16[4,128,256]{2,1,0:T(8,128)(2,1)S(1)} %bands.3.right_ref.rest_1_), channel_id=1, source_target_pairs={{0,24},{8,0},{16,8},{24,16},{1,25},{9,1},{17,9},{25,17},{2,26},{10... | collective-permute-start | bytes 786440 | tf_op jit(solution)/shard_map/ppermute | solution.py:497
  32.5 0.0 collective-permute-done.17.rest_3_
  32.5 0.0 collective-permute-start.18
  32.5 0.3 left.3.rest_0_
  32.9 3.9 %collective-permute-start.9 = (bf16[4,128,256]{2,1,0:T(8,128)(2,1)S(1)}, bf16[4,128,256]{2,1,0:T(8,128)(2,1)S(1)}, u32[]{:S(2)}, u32[]{:S(2)}) collective-permute-start(bf16[4,128,256]{2,1,0:T(8,128)(2,1)S(1)} %bands.2.right_ref.rest_2_), channel_id=1, source_target_pairs={{0,24},{8,0},{16,8},{24,16},{1,25},{9,1},{17,9},{25,17},{2,26},{10... | collective-permute-start | bytes 786440 | tf_op jit(solution)/shard_map/ppermute | solution.py:497
  36.8 3.6 %correlate.5.rest_5_ = f32[4,8,2,256,1024]{4,3,2,1,0:T(8,128)} custom-call(s32[1]{0:T(128)} %bitcast.me_ref, bf16[2,4,256,128]{3,2,1,0:T(8,128)(2,1)S(1)} %left.3.rest_0_, bf16[4,128,256]{2,1,0:T(8,128)(2,1)S(1)} %bands.3.right_ref.rest_1_), custom_call_target="tpu_custom_call" | custom-call | flops 536870912 | bytes 8388608 | tf_op jit(solution)/shard_map/correlate/pallas_call | solution.py:446
  40.4 0.3 left.2.rest_1_.rest_0_
  40.7 0.0 collective-permute-done.7.rest_3_
  40.7 3.0 %collective-permute-start.8 = (bf16[4,128,256]{2,1,0:T(8,128)(2,1)S(1)}, bf16[4,128,256]{2,1,0:T(8,128)(2,1)S(1)}, u32[]{:S(2)}, u32[]{:S(2)}) collective-permute-start(bf16[4,128,256]{2,1,0:T(8,128)(2,1)S(1)} %collective-permute-done.7.rest_3_), channel_id=1, source_target_pairs={{0,8},{8,16},{16,24},{24,0},{1,9},{9,17},{17,25},{25,1},{2,10},{10... | collective-permute-start | bytes 786440 | tf_op jit(solution)/shard_map/ppermute | solution.py:498
  43.7 1.7 %collective-permute-done.19.rest_4_ = bf16[4,128,256]{2,1,0:T(8,128)(2,1)S(1)} collective-permute-done((bf16[4,128,256]{2,1,0:T(8,128)(2,1)S(1)}, bf16[4,128,256]{2,1,0:T(8,128)(2,1)S(1)}, u32[]{:S(2)}, u32[]{:S(2)}) %collective-permute-start.19) | collective-permute-done | bytes 262176 | tf_op jit(solution)/shard_map/ppermute | solution.py:497
  45.4 8.7 %correlate.6.rest_4_ = f32[4,8,2,256,1024]{4,3,2,1,0:T(8,128)} custom-call(s32[1]{0:T(128)} %bitcast.me_ref, bf16[2,4,256,128]{3,2,1,0:T(8,128)(2,1)S(1)} %left.3.rest_0_, bf16[2,4,256,128]{3,2,1,0:T(8,128)(2,1)S(1)} %left.2.rest_1_.rest_0_, bf16[4,128,256]{2,1,0:T(8,128)(2,1)S(1)} %bands.2.right_ref.rest_2_, ...), custom_call_target="tpu_custom_call", output_to_operand_aliasing={{}: (6, {})} | custom-call | flops 1610612736 | bytes 25165824 | tf_op jit(solution)/shard_map/correlate/pallas_call | solution.py:446
  54.1 0.0 collective-permute-done.18.rest_2_
  54.1 6.2 %correlate.7.rest_2_ = f32[4,8,2,256,1024]{4,3,2,1,0:T(8,128)} custom-call(s32[1]{0:T(128)} %bitcast.me_ref, bf16[2,4,256,128]{3,2,1,0:T(8,128)(2,1)S(1)} %left.3.rest_0_, bf16[2,4,256,128]{3,2,1,0:T(8,128)(2,1)S(1)} %left.2.rest_1_.rest_0_, bf16[4,128,256]{2,1,0:T(8,128)(2,1)S(1)} %collective-permute-done.18.rest_2_, ...), custom_call_target="tpu_custom_call", output_to_operand_aliasing={{}: (5, {})} | custom-call | flops 1073741824 | bytes 16777216 | tf_op jit(solution)/shard_map/correlate/pallas_call | solution.py:446
  60.3 0.0 collective-permute-done.9.rest_1_
  60.3 3.6 %correlate.8.rest_2_ = f32[4,8,2,256,1024]{4,3,2,1,0:T(8,128)} custom-call(s32[1]{0:T(128)} %bitcast.me_ref, bf16[2,4,256,128]{3,2,1,0:T(8,128)(2,1)S(1)} %left.2.rest_1_.rest_0_, bf16[4,128,256]{2,1,0:T(8,128)(2,1)S(1)} %collective-permute-done.9.rest_1_, f32[4,8,2,256,1024]{4,3,2,1,0:T(8,128)} %correlate.7.rest_2_), custom_call_target="tpu_custom_call", output_to_operand_aliasing={{}: (3, {})} | custom-call | flops 536870912 | bytes 8388608 | tf_op jit(solution)/shard_map/correlate/pallas_call | solution.py:446
  63.9 0.0 collective-permute-done.8.rest_1_
  63.9 3.6 %correlate.9 = f32[4,8,2,256,1024]{4,3,2,1,0:T(8,128)} custom-call(s32[1]{0:T(128)} %bitcast.me_ref, bf16[2,4,256,128]{3,2,1,0:T(8,128)(2,1)S(1)} %left.2.rest_1_.rest_0_, bf16[4,128,256]{2,1,0:T(8,128)(2,1)S(1)} %collective-permute-done.8.rest_1_, f32[4,8,2,256,1024]{4,3,2,1,0:T(8,128)} %correlate.8.rest_2_), custom_call_target="tpu_custom_call", output_to_operand_aliasing={{}: (3, {})} | custom-call | flops 536870912 | bytes 8388608 | tf_op jit(solution)/shard_map/correlate/pallas_call | solution.py:446
Async XLA Ops:
  5.5 4.9 %collective-permute-start.10 = (bf16[8,16,256]{2,1,0:T(8,128)(2,1)S(1)}, bf16[8,16,256]{2,1,0:T(8,128)(2,1)S(1)}, u32[]{:S(2)}, u32[]{:S(2)}) collective-permute-start(bf16[8,16,256]{2,1,0:T(8,128)(2,1)S(1)} %get-tuple-element.32), channel_id=1, source_target_pairs={{0,1},{1,0},{2,3},{3,2},{4,5},{5,4},{6,7},{7,6},{8,9},{9,8},{10,11... | collective-permute-start | bytes 196616 | tf_op jit(solution)/shard_map/ppermute | solution.py:484
  6.0 7.0 %collective-permute-start.11 = (bf16[8,16,256]{2,1,0:T(8,128)(2,1)S(1)}, bf16[8,16,256]{2,1,0:T(8,128)(2,1)S(1)}, u32[]{:S(2)}, u32[]{:S(2)}) collective-permute-start(bf16[8,16,256]{2,1,0:T(8,128)(2,1)S(1)} %get-tuple-element.33), channel_id=1, source_target_pairs={{0,2},{1,3},{2,0},{3,1},{4,6},{5,7},{6,4},{7,5},{8,10},{9,11},{10,... | collective-permute-start | bytes 196616 | tf_op jit(solution)/shard_map/ppermute | solution.py:484
  8.6 6.3 %collective-permute-start.12 = (bf16[8,16,256]{2,1,0:T(8,128)(2,1)S(1)}, bf16[8,16,256]{2,1,0:T(8,128)(2,1)S(1)}, u32[]{:S(2)}, u32[]{:S(2)}) collective-permute-start(bf16[8,16,256]{2,1,0:T(8,128)(2,1)S(1)} %get-tuple-element.34), channel_id=1, source_target_pairs={{0,3},{1,2},{2,1},{3,0},{4,7},{5,6},{6,5},{7,4},{8,11},{9,10},{10,... | collective-permute-start | bytes 196616 | tf_op jit(solution)/shard_map/ppermute | solution.py:484
  8.6 7.8 %collective-permute-start.13 = (bf16[8,16,256]{2,1,0:T(8,128)(2,1)S(1)}, bf16[8,16,256]{2,1,0:T(8,128)(2,1)S(1)}, u32[]{:S(2)}, u32[]{:S(2)}) collective-permute-start(bf16[8,16,256]{2,1,0:T(8,128)(2,1)S(1)} %get-tuple-element.35), channel_id=1, source_target_pairs={{0,4},{1,5},{2,6},{3,7},{4,0},{5,1},{6,2},{7,3},{8,12},{9,13},{10,... | collective-permute-start | bytes 196616 | tf_op jit(solution)/shard_map/ppermute | solution.py:484
  10.4 6.5 %collective-permute-start.14 = (bf16[8,16,256]{2,1,0:T(8,128)(2,1)S(1)}, bf16[8,16,256]{2,1,0:T(8,128)(2,1)S(1)}, u32[]{:S(2)}, u32[]{:S(2)}) collective-permute-start(bf16[8,16,256]{2,1,0:T(8,128)(2,1)S(1)} %get-tuple-element.36), channel_id=1, source_target_pairs={{0,5},{1,4},{2,7},{3,6},{4,1},{5,0},{6,3},{7,2},{8,13},{9,12},{10,... | collective-permute-start | bytes 196616 | tf_op jit(solution)/shard_map/ppermute | solution.py:484
  10.4 8.1 %collective-permute-start.15 = (bf16[8,16,256]{2,1,0:T(8,128)(2,1)S(1)}, bf16[8,16,256]{2,1,0:T(8,128)(2,1)S(1)}, u32[]{:S(2)}, u32[]{:S(2)}) collective-permute-start(bf16[8,16,256]{2,1,0:T(8,128)(2,1)S(1)} %get-tuple-element.37), channel_id=1, source_target_pairs={{0,6},{1,7},{2,4},{3,5},{4,2},{5,3},{6,0},{7,1},{8,14},{9,15},{10,... | collective-permute-start | bytes 196616 | tf_op jit(solution)/shard_map/ppermute | solution.py:484
  13.0 5.5 %collective-permute-start.16 = (bf16[8,16,256]{2,1,0:T(8,128)(2,1)S(1)}, bf16[8,16,256]{2,1,0:T(8,128)(2,1)S(1)}, u32[]{:S(2)}, u32[]{:S(2)}) collective-permute-start(bf16[8,16,256]{2,1,0:T(8,128)(2,1)S(1)} %get-tuple-element.38), channel_id=1, source_target_pairs={{0,7},{1,6},{2,5},{3,4},{4,3},{5,2},{6,1},{7,0},{8,15},{9,14},{10,... | collective-permute-start | bytes 196616 | tf_op jit(solution)/shard_map/ppermute | solution.py:484
  14.9 7.1 %collective-permute-start = (bf16[8,16,256]{2,1,0:T(8,128)(2,1)S(1)}, bf16[8,16,256]{2,1,0:T(8,128)(2,1)S(1)}, u32[]{:S(2)}, u32[]{:S(2)}) collective-permute-start(bf16[8,16,256]{2,1,0:T(8,128)(2,1)S(1)} %get-tuple-element.24), channel_id=1, source_target_pairs={{0,1},{1,0},{2,3},{3,2},{4,5},{5,4},{6,7},{7,6},{8,9},{9,8},{10,11... | collective-permute-start | bytes 196616 | tf_op jit(solution)/shard_map/ppermute | solution.py:484
  16.4 5.6 %collective-permute-start.1 = (bf16[8,16,256]{2,1,0:T(8,128)(2,1)S(1)}, bf16[8,16,256]{2,1,0:T(8,128)(2,1)S(1)}, u32[]{:S(2)}, u32[]{:S(2)}) collective-permute-start(bf16[8,16,256]{2,1,0:T(8,128)(2,1)S(1)} %get-tuple-element.25), channel_id=1, source_target_pairs={{0,2},{1,3},{2,0},{3,1},{4,6},{5,7},{6,4},{7,5},{8,10},{9,11},{10,... | collective-permute-start | bytes 196616 | tf_op jit(solution)/shard_map/ppermute | solution.py:484
  16.9 6.1 %collective-permute-start.2 = (bf16[8,16,256]{2,1,0:T(8,128)(2,1)S(1)}, bf16[8,16,256]{2,1,0:T(8,128)(2,1)S(1)}, u32[]{:S(2)}, u32[]{:S(2)}) collective-permute-start(bf16[8,16,256]{2,1,0:T(8,128)(2,1)S(1)} %get-tuple-element.26), channel_id=1, source_target_pairs={{0,3},{1,2},{2,1},{3,0},{4,7},{5,6},{6,5},{7,4},{8,11},{9,10},{10,... | collective-permute-start | bytes 196616 | tf_op jit(solution)/shard_map/ppermute | solution.py:484
  18.8 13.8 %collective-permute-start.17 = (bf16[4,128,256]{2,1,0:T(8,128)(2,1)S(1)}, bf16[4,128,256]{2,1,0:T(8,128)(2,1)S(1)}, u32[]{:S(2)}, u32[]{:S(2)}) collective-permute-start(bf16[4,128,256]{2,1,0:T(8,128)(2,1)S(1)} %bands.3.right_ref.rest_1_), channel_id=1, source_target_pairs={{0,8},{8,16},{16,24},{24,0},{1,9},{9,17},{17,25},{25,1},{2,10},{10... | collective-permute-start | bytes 786440 | tf_op jit(solution)/shard_map/ppermute | solution.py:496
  20.4 4.4 %collective-permute-start.3 = (bf16[8,16,256]{2,1,0:T(8,128)(2,1)S(1)}, bf16[8,16,256]{2,1,0:T(8,128)(2,1)S(1)}, u32[]{:S(2)}, u32[]{:S(2)}) collective-permute-start(bf16[8,16,256]{2,1,0:T(8,128)(2,1)S(1)} %get-tuple-element.27), channel_id=1, source_target_pairs={{0,4},{1,5},{2,6},{3,7},{4,0},{5,1},{6,2},{7,3},{8,12},{9,13},{10,... | collective-permute-start | bytes 196616 | tf_op jit(solution)/shard_map/ppermute | solution.py:484
  22.0 5.9 %collective-permute-start.4 = (bf16[8,16,256]{2,1,0:T(8,128)(2,1)S(1)}, bf16[8,16,256]{2,1,0:T(8,128)(2,1)S(1)}, u32[]{:S(2)}, u32[]{:S(2)}) collective-permute-start(bf16[8,16,256]{2,1,0:T(8,128)(2,1)S(1)} %get-tuple-element.28), channel_id=1, source_target_pairs={{0,5},{1,4},{2,7},{3,6},{4,1},{5,0},{6,3},{7,2},{8,13},{9,12},{10,... | collective-permute-start | bytes 196616 | tf_op jit(solution)/shard_map/ppermute | solution.py:484
  22.0 6.0 %collective-permute-start.5 = (bf16[8,16,256]{2,1,0:T(8,128)(2,1)S(1)}, bf16[8,16,256]{2,1,0:T(8,128)(2,1)S(1)}, u32[]{:S(2)}, u32[]{:S(2)}) collective-permute-start(bf16[8,16,256]{2,1,0:T(8,128)(2,1)S(1)} %get-tuple-element.29), channel_id=1, source_target_pairs={{0,6},{1,7},{2,4},{3,5},{4,2},{5,3},{6,0},{7,1},{8,14},{9,15},{10,... | collective-permute-start | bytes 196616 | tf_op jit(solution)/shard_map/ppermute | solution.py:484
  23.0 5.4 %collective-permute-start.6 = (bf16[8,16,256]{2,1,0:T(8,128)(2,1)S(1)}, bf16[8,16,256]{2,1,0:T(8,128)(2,1)S(1)}, u32[]{:S(2)}, u32[]{:S(2)}) collective-permute-start(bf16[8,16,256]{2,1,0:T(8,128)(2,1)S(1)} %get-tuple-element.30), channel_id=1, source_target_pairs={{0,7},{1,6},{2,5},{3,4},{4,3},{5,2},{6,1},{7,0},{8,15},{9,14},{10,... | collective-permute-start | bytes 196616 | tf_op jit(solution)/shard_map/ppermute | solution.py:484
  28.7 12.1 %collective-permute-start.7 = (bf16[4,128,256]{2,1,0:T(8,128)(2,1)S(1)}, bf16[4,128,256]{2,1,0:T(8,128)(2,1)S(1)}, u32[]{:S(2)}, u32[]{:S(2)}) collective-permute-start(bf16[4,128,256]{2,1,0:T(8,128)(2,1)S(1)} %bands.2.right_ref.rest_2_), channel_id=1, source_target_pairs={{0,8},{8,16},{16,24},{24,0},{1,9},{9,17},{17,25},{25,1},{2,10},{10... | collective-permute-start | bytes 786440 | tf_op jit(solution)/shard_map/ppermute | solution.py:496
  30.3 15.1 %collective-permute-start.19 = (bf16[4,128,256]{2,1,0:T(8,128)(2,1)S(1)}, bf16[4,128,256]{2,1,0:T(8,128)(2,1)S(1)}, u32[]{:S(2)}, u32[]{:S(2)}) collective-permute-start(bf16[4,128,256]{2,1,0:T(8,128)(2,1)S(1)} %bands.3.right_ref.rest_1_), channel_id=1, source_target_pairs={{0,24},{8,0},{16,8},{24,16},{1,25},{9,1},{17,9},{25,17},{2,26},{10... | collective-permute-start | bytes 786440 | tf_op jit(solution)/shard_map/ppermute | solution.py:497
  32.5 21.5 %collective-permute-start.18 = (bf16[4,128,256]{2,1,0:T(8,128)(2,1)S(1)}, bf16[4,128,256]{2,1,0:T(8,128)(2,1)S(1)}, u32[]{:S(2)}, u32[]{:S(2)}) collective-permute-start(bf16[4,128,256]{2,1,0:T(8,128)(2,1)S(1)} %collective-permute-done.17.rest_3_), channel_id=1, source_target_pairs={{0,8},{8,16},{16,24},{24,0},{1,9},{9,17},{17,25},{25,1},{2,10},{10... | collective-permute-start | bytes 786440 | tf_op jit(solution)/shard_map/ppermute | solution.py:498
  32.9 27.4 %collective-permute-start.9 = (bf16[4,128,256]{2,1,0:T(8,128)(2,1)S(1)}, bf16[4,128,256]{2,1,0:T(8,128)(2,1)S(1)}, u32[]{:S(2)}, u32[]{:S(2)}) collective-permute-start(bf16[4,128,256]{2,1,0:T(8,128)(2,1)S(1)} %bands.2.right_ref.rest_2_), channel_id=1, source_target_pairs={{0,24},{8,0},{16,8},{24,16},{1,25},{9,1},{17,9},{25,17},{2,26},{10... | collective-permute-start | bytes 786440 | tf_op jit(solution)/shard_map/ppermute | solution.py:497
  40.7 23.2 %collective-permute-start.8 = (bf16[4,128,256]{2,1,0:T(8,128)(2,1)S(1)}, bf16[4,128,256]{2,1,0:T(8,128)(2,1)S(1)}, u32[]{:S(2)}, u32[]{:S(2)}) collective-permute-start(bf16[4,128,256]{2,1,0:T(8,128)(2,1)S(1)} %collective-permute-done.7.rest_3_), channel_id=1, source_target_pairs={{0,8},{8,16},{16,24},{24,0},{1,9},{9,17},{17,25},{25,1},{2,10},{10... | collective-permute-start | bytes 786440 | tf_op jit(solution)/shard_map/ppermute | solution.py:498

commit v4 on v3

--- a/solution.py
+++ b/solution.py
@@ -258,8 +258,8 @@
 
 
 def next_kernel(half, dests, place_ref, y, far_ref, row_ref, low_ref, *rest):
-    outs = rest[:dests]
-    table, far, row, low, sems = rest[dests:]
+    keep, give, (table, far, row, low, sems) = rest[: dests // 2], rest[dests // 2], rest[dests // 2 + 1 :]
+    outs = [keep[k // 2] if k % 2 == 0 else give.at[k // 2] for k in range(dests)]
     me = place_ref[0]
     small = table_copies(half, me, far_ref, row_ref, low_ref, far, row, low, sems)
     for load in small:
@@ -276,11 +276,12 @@
     radix = slots // LANES
     rows = LANES // dests // HALVES
     far, row, low = branch_tables(phases, radix, dests)
-    parts = 8
+    parts = 16
     here = far.shape[1] // HALVES
     whole, near = pl.BlockSpec(memory_space=pl.ANY), pl.BlockSpec(memory_space=pltpu.VMEM)
     place = pl.BlockSpec(memory_space=pltpu.SMEM)
     blocks = [pltpu.VMEM((radix, 2 * rows, inputs), jnp.bfloat16)] * dests
+    give = pltpu.VMEM((dests // 2, radix, 2 * rows, inputs), jnp.bfloat16)
     y = pltpu.VMEM((radix // 2 + 1, 2, 2 * LANES, inputs), jnp.bfloat16)
     table = pltpu.VMEM((2, radix, here, 2 * LANES), jnp.bfloat16)
     small = [
@@ -312,9 +313,9 @@
         result.append(
             pl.pallas_call(
                 functools.partial(next_kernel, half, dests),
-                out_shape=blocks,
+                out_shape=blocks[: dests // 2] + [give],
                 in_specs=[place, near] + [whole] * 3,
-                out_specs=[near] * dests,
+                out_specs=[near] * (dests // 2 + 1),
                 scratch_shapes=[table] + small + [pltpu.SemaphoreType.DMA((3,))],
                 cost_estimate=pl.CostEstimate(flops=flops, transcendentals=0, bytes_accessed=4 * far.size),
                 name="branch_next",
@@ -339,8 +340,33 @@
     return in_order(pieces, me, bit + 1)
 
 
+def join_kernel(*refs):
+    count = len(refs) // 2
+    keep, got, outs = refs[:count], refs[count], refs[count + 1 :]
+    for m, out_ref in enumerate(outs):
+        out_ref[0] = keep[m][...]
+        out_ref[1] = got[m + 1]
+
+
+def join(keep, got):
+    shape = keep[0].shape
+    near = pl.BlockSpec(memory_space=pltpu.VMEM)
+    return pl.pallas_call(
+        join_kernel,
+        out_shape=[pltpu.VMEM((2,) + shape, keep[0].dtype)] * len(keep),
+        in_specs=[near] * (len(keep) + 1),
+        out_specs=[near] * len(keep),
+        name="join",
+    )(*keep, got)
+
+
 def band_kernel(place_ref, *rest):
-    blocks, out_ref = rest[:-1], rest[-1]
+    out_ref, blocks = rest[-1], []
+    for ref in rest[:-1]:
+        if len(ref.shape) == 3:
+            blocks.append(ref)
+        else:
+            blocks += [ref.at[0]] if ref.shape[0] > 2 else [ref.at[0], ref.at[1]]
     phases = len(blocks)
     radix, rows, _ = blocks[0].shape
     near, half = rows // 2, phases // 2
@@ -357,14 +383,13 @@
             out_ref[c, u * rows : (u + 1) * rows] = jnp.concatenate(spectrum, axis=0).astype(jnp.bfloat16)
 
 
-def bands_of(blocks, me):
-    phases = len(blocks)
+def bands_of(blocks, me, phases):
     radix, rows, inputs = blocks[0].shape
     bands, depth = phases // 2, radix * rows
     return pl.pallas_call(
         band_kernel,
         out_shape=pltpu.VMEM((bands, depth, inputs), jnp.bfloat16),
-        in_specs=[pl.BlockSpec(memory_space=pltpu.SMEM)] + [pl.BlockSpec(memory_space=pltpu.VMEM)] * phases,
+        in_specs=[pl.BlockSpec(memory_space=pltpu.SMEM)] + [pl.BlockSpec(memory_space=pltpu.VMEM)] * len(blocks),
         out_specs=pl.BlockSpec(memory_space=pltpu.VMEM),
         cost_estimate=pl.CostEstimate(flops=0, transcendentals=0, bytes_accessed=6 * bands * depth * inputs),
         name="bands",
@@ -479,10 +504,16 @@
     own, lefts = [], []
     for h in range(HALVES):
         blocks = list(branch[h])
-        for k in range(1, dests):
+        if h > 0:
+            keep, got = blocks[:-1], lax.ppermute(blocks[-1], "chan", [(i, i ^ 1) for i in range(dests)])
+            got = near_memory(got)
+            pairs = join(keep[1:], got)
+            blocks = [keep[0], got] + [near_memory(x) for x in pairs]
+        for at in range(1 if h == 0 else 2, len(blocks)):
+            k = at if h == 0 else 2 * (at - 1)
             route = [(i, i ^ k) for i in range(dests)]
-            blocks[k] = near_memory(lax.ppermute(blocks[k], "chan", route))
-        own.append(near_memory(bands_of(blocks, place)))
+            blocks[at] = near_memory(lax.ppermute(blocks[at], "chan", route))
+        own.append(near_memory(bands_of(blocks, place, phases)))
         lefts.append(near_memory(left_of(own[h], near)))
     me = lax.axis_index("stn")
     stations = lax.axis_size("stn")
@@ -496,11 +527,17 @@
         first.append(near_memory(lax.ppermute(x, "stn", onward)))
         last.append(near_memory(lax.ppermute(x, "stn", backward)))
         second.append(near_memory(lax.ppermute(first[h], "stn", onward)))
-    total = add([(0, 0, own[0])], total=None)
-    total = add([(1, 0, own[1]), (0, 1, first[0]), (0, 3, last[0])], total=total)
-    total = add([(0, 2, second[0]), (1, 1, first[1])], total=total)
-    total = add([(1, 3, last[1])], total=total)
-    total = add([(1, 2, second[1])], total=total)
+    jobs = (
+        [(0, 0, own[0])],
+        [(1, 0, own[1]), (0, 1, first[0])],
+        [(0, 3, last[0]), (1, 1, first[1])],
+        [(0, 2, second[0])],
+        [(1, 3, last[1])],
+        [(1, 2, second[1])],
+    )
+    total = None
+    for job in jobs:
+        total = add(job, total=total)
     return total
 
 
@@ -513,7 +550,7 @@
         lanes == phases
         and frames == tap_count
         and phases & (phases - 1) == 0
-        and phases % 2 == 0
+        and phases > 4
         and slots % LANES == 0
         and radix % 2 == 0
         and AVG % radix == 0

time: 67.7 us -> 73.2 us (1.081)
  waiting for transfers between devices: 5.31 us -> 11.4 us
  starting transfers between devices: 28.1 us -> 23.6 us
  Pallas kernels: 34 us -> 37.3 us
    ppermute x2, waiting for transfers between devices: 0.01 us -> 5.58 us  [one_frame(): first.append(near_memory(lax.ppermute(x, 'stn', onward)))]
    pallas_call x5 -> x6, Pallas kernels: 25.7 us -> 28.7 us  [correlate(): pl.pallas_call(functools.partial(correlate_kernel, near, group, listed, s...]
    ppermute x14 -> x11, starting transfers between devices: 15.7 us -> 13.3 us  [the longest x10 12.7 us: one_frame(): blocks[at] = near_memory(lax.ppermute(blocks[at], 'chan', route))]
    ppermute x14 -> x11, waiting for transfers between devices: 3.63 us -> 5.8 us  [the longest x10 5.8 us: one_frame(): blocks[at] = near_memory(lax.ppermute(blocks[at], 'chan', route))]
    ppermute x2, starting transfers between devices: 3.01 us -> 1.16 us  [one_frame(): second.append(near_memory(lax.ppermute(first[h], 'stn', onward)))]
    ppermute x2, waiting for transfers between devices: 1.67 us -> 0.01 us  [one_frame(): last.append(near_memory(lax.ppermute(x, 'stn', backward)))]
  transfers between devices with their start and end apart: 20 -> 17, of which waited for: 4 -> 4; matrix products, arithmetic and copies ran while one was open for 0% -> 0% of each run, Pallas kernels for 37% -> 35%
where the time goes in v4:
time: 73.2 us; the launch traced here: 72.5 us
  Pallas kernels  37.3 us (51%)
  starting transfers between devices  23.6 us (32%)
  waiting for transfers between devices  11.4 us (16%)
    pallas_call x6, Pallas kernels, correlate(): pl.pallas_call(functools.partial(correlate_kernel, near, group, listed, s...  28.7 us
    ppermute x10, starting transfers between devices, one_frame(): blocks[at] = near_memory(lax.ppermute(blocks[at], 'chan', route))  12.7 us
    ppermute x2, starting transfers between devices, one_frame(): last.append(near_memory(lax.ppermute(x, 'stn', backward)))  6.12 us
    ppermute x10, waiting for transfers between devices, one_frame(): blocks[at] = near_memory(lax.ppermute(blocks[at], 'chan', route))  5.8 us
    pallas_call x1, Pallas kernels, branch_of(): pl.pallas_call(functools.partial(first_kernel, radix, dests), out_shape=b...  5.69 us
    ppermute x2, waiting for transfers between devices, one_frame(): first.append(near_memory(lax.ppermute(x, 'stn', onward)))  5.58 us
    ppermute x2, starting transfers between devices, one_frame(): first.append(near_memory(lax.ppermute(x, 'stn', onward)))  3.03 us
    pallas_call x1, Pallas kernels, branch_of(): pl.pallas_call(functools.partial(next_kernel, half, dests), out_shape=blo...  1.7 us
  transfers between devices with their start and end apart: 17, of which 4 were waited for; matrix products, arithmetic and copies ran while one was open for 0% of the time, Pallas kernels for 35%

profile of v4, /device:TPU:0, one launch (start us, length us, event | category | flops | bytes accessed | tf_op | source)
XLA Modules:
  0.0 72.5 jit_solution(13525799936157242795)
XLA Ops:
  0.0 5.7 %branch.1 = (bf16[8,16,256]{2,1,0:T(8,128)(2,1)S(1)}, bf16[8,16,256]{2,1,0:T(8,128)(2,1)S(1)}, bf16[8,16,256]{2,1,0:T(8,128)(2,1)S(1)}, bf16[8,16,256]{2,1,0:T(8...) custom-call(s32[1]{0:T(128)} %bitcast.1.place_ref, ...), custom_call_target="tpu_custom_call" | custom-call | flops 402653184 | bytes 4194304 | tf_op jit(solution)/shard_map/branch/pallas_call | solution.py:293
  5.7 1.7 %branch_next.1 = (bf16[8,16,256]{2,1,0:T(8,128)(2,1)S(1)}, bf16[8,16,256]{2,1,0:T(8,128)(2,1)S(1)}, bf16[8,16,256]{2,1,0:T(8,128)(2,1)S(1)}, bf16[8,16,256]{2,1,0:T(8,128)(2,1)S(1)}, bf16[4,8,16,256]{3,2,1,0:T(8,128)(2,1)S(1)}) custom-call(s32[1]{0:T(128)} %bitcast.1.place_ref, bf16[5,2,256,256]{3,2,1,0:T(8,128)(2,1)S(1)} %get-tuple-element.22.y, ...), custom_call_target="tpu_custom_call" | custom-call | flops 402653184 | bytes 524288 | tf_op jit(solution)/shard_map/branch_next/pallas_call | solution.py:314
  7.4 0.6 collective-permute-start
  8.0 2.5 %collective-permute-start.10 = (bf16[8,16,256]{2,1,0:T(8,128)(2,1)S(1)}, bf16[8,16,256]{2,1,0:T(8,128)(2,1)S(1)}, u32[]{:S(2)}, u32[]{:S(2)}) collective-permute-start(bf16[8,16,256]{2,1,0:T(8,128)(2,1)S(1)} %get-tuple-element.35), channel_id=1, source_target_pairs={{0,4},{1,5},{2,6},{3,7},{4,0},{5,1},{6,2},{7,3},{8,12},{9,13},{10,... | collective-permute-start | bytes 196616 | tf_op jit(solution)/shard_map/ppermute | solution.py:515
  10.6 0.0 collective-permute-start.11
  10.6 2.7 %collective-permute-start.12 = (bf16[8,16,256]{2,1,0:T(8,128)(2,1)S(1)}, bf16[8,16,256]{2,1,0:T(8,128)(2,1)S(1)}, u32[]{:S(2)}, u32[]{:S(2)}) collective-permute-start(bf16[8,16,256]{2,1,0:T(8,128)(2,1)S(1)} %get-tuple-element.37), channel_id=1, source_target_pairs={{0,6},{1,7},{2,4},{3,5},{4,2},{5,3},{6,0},{7,1},{8,14},{9,15},{10,... | collective-permute-start | bytes 196616 | tf_op jit(solution)/shard_map/ppermute | solution.py:515
  13.3 0.0 collective-permute-start.13
  13.3 0.0 collective-permute-done.refs_3_.rest_1_
  13.3 0.4 collective-permute-start.7
  13.7 0.0 collective-permute-done.10.rest_4_
  13.7 1.8 %collective-permute-start.1 = (bf16[2,8,16,256]{3,2,1,0:T(8,128)(2,1)S(1)}, bf16[2,8,16,256]{3,2,1,0:T(8,128)(2,1)S(1)}, u32[]{:S(2)}, u32[]{:S(2)}) collective-permute-start(bf16[2,8,16,256]{3,2,1,0:T(8,128)(2,1)S(1)} %get-tuple-element.28), channel_id=1, source_target_pairs={{0,2},{1,3},{2,0},{3,1},{4,6},{5,7},{6,4},{7,5},{8,10},{9,11},{10,... | collective-permute-start | bytes 393224 | tf_op jit(solution)/shard_map/ppermute | solution.py:515
  15.5 0.5 collective-permute-done.11.rest_5_
  16.0 1.0 %collective-permute-start.2 = (bf16[2,8,16,256]{3,2,1,0:T(8,128)(2,1)S(1)}, bf16[2,8,16,256]{3,2,1,0:T(8,128)(2,1)S(1)}, u32[]{:S(2)}, u32[]{:S(2)}) collective-permute-start(bf16[2,8,16,256]{3,2,1,0:T(8,128)(2,1)S(1)} %get-tuple-element.29), channel_id=1, source_target_pairs={{0,4},{1,5},{2,6},{3,7},{4,0},{5,1},{6,2},{7,3},{8,12},{9,13},{10,... | collective-permute-start | bytes 393224 | tf_op jit(solution)/shard_map/ppermute | solution.py:515
  17.0 0.0 collective-permute-done.12.rest_6_
  17.0 2.2 %collective-permute-start.3 = (bf16[2,8,16,256]{3,2,1,0:T(8,128)(2,1)S(1)}, bf16[2,8,16,256]{3,2,1,0:T(8,128)(2,1)S(1)}, u32[]{:S(2)}, u32[]{:S(2)}) collective-permute-start(bf16[2,8,16,256]{3,2,1,0:T(8,128)(2,1)S(1)} %get-tuple-element.30), channel_id=1, source_target_pairs={{0,6},{1,7},{2,4},{3,5},{4,2},{5,3},{6,0},{7,1},{8,14},{9,15},{10,... | collective-permute-start | bytes 393224 | tf_op jit(solution)/shard_map/ppermute | solution.py:515
  19.2 0.0 collective-permute-done.13.rest_7_
  19.2 0.3 collective-permute-start.8
  19.5 0.0 collective-permute-done.7.rest_1_
  19.5 1.8 %collective-permute-start.9 = (bf16[8,16,256]{2,1,0:T(8,128)(2,1)S(1)}, bf16[8,16,256]{2,1,0:T(8,128)(2,1)S(1)}, u32[]{:S(2)}, u32[]{:S(2)}) collective-permute-start(bf16[8,16,256]{2,1,0:T(8,128)(2,1)S(1)} %get-tuple-element.34), channel_id=1, source_target_pairs={{0,3},{1,2},{2,1},{3,0},{4,7},{5,6},{6,5},{7,4},{8,11},{9,10},{10,... | collective-permute-start | bytes 196616 | tf_op jit(solution)/shard_map/ppermute | solution.py:515
  21.3 4.0 %collective-permute-done.8.rest_2_ = bf16[8,16,256]{2,1,0:T(8,128)(2,1)S(1)} collective-permute-done((bf16[8,16,256]{2,1,0:T(8,128)(2,1)S(1)}, bf16[8,16,256]{2,1,0:T(8,128)(2,1)S(1)}, u32[]{:S(2)}, u32[]{:S(2)}) %collective-permute-start.8) | collective-permute-done | bytes 65568 | tf_op jit(solution)/shard_map/ppermute | solution.py:515
  25.3 1.3 %collective-permute-done.9.rest_3_ = bf16[8,16,256]{2,1,0:T(8,128)(2,1)S(1)} collective-permute-done((bf16[8,16,256]{2,1,0:T(8,128)(2,1)S(1)}, bf16[8,16,256]{2,1,0:T(8,128)(2,1)S(1)}, u32[]{:S(2)}, u32[]{:S(2)}) %collective-permute-start.9) | collective-permute-done | bytes 65568 | tf_op jit(solution)/shard_map/ppermute | solution.py:515
  26.6 0.2 bands.3.right_ref.rest_1_
  26.8 1.4 %collective-permute-start.14 = (bf16[4,128,256]{2,1,0:T(8,128)(2,1)S(1)}, bf16[4,128,256]{2,1,0:T(8,128)(2,1)S(1)}, u32[]{:S(2)}, u32[]{:S(2)}) collective-permute-start(bf16[4,128,256]{2,1,0:T(8,128)(2,1)S(1)} %bands.3.right_ref.rest_1_), channel_id=1, source_target_pairs={{0,8},{8,16},{16,24},{24,0},{1,9},{9,17},{17,25},{25,1},{2,10},{10... | collective-permute-start | bytes 786440 | tf_op jit(solution)/shard_map/ppermute | solution.py:527
  28.2 0.0 collective-permute-done.1.rest_2_
  28.2 0.0 collective-permute-done.2.rest_3_
  28.2 0.0 collective-permute-done.3.rest_4_
  28.2 0.3 bands.2.right_ref.rest_2_
  28.5 1.6 %collective-permute-start.4 = (bf16[4,128,256]{2,1,0:T(8,128)(2,1)S(1)}, bf16[4,128,256]{2,1,0:T(8,128)(2,1)}, u32[]{:S(2)}, u32[]{:S(2)}) collective-permute-start(bf16[4,128,256]{2,1,0:T(8,128)(2,1)S(1)} %bands.2.right_ref.rest_2_), channel_id=1, source_target_pairs={{0,8},{8,16},{16,24},{24,0},{1,9},{9,17},{17,25},{25,1},{2,10},{10... | collective-permute-start | bytes 786440 | tf_op jit(solution)/shard_map/ppermute | solution.py:527
  30.1 2.2 %collective-permute-start.16 = (bf16[4,128,256]{2,1,0:T(8,128)(2,1)S(1)}, bf16[4,128,256]{2,1,0:T(8,128)(2,1)S(1)}, u32[]{:S(2)}, u32[]{:S(2)}) collective-permute-start(bf16[4,128,256]{2,1,0:T(8,128)(2,1)S(1)} %bands.3.right_ref.rest_1_), channel_id=1, source_target_pairs={{0,24},{8,0},{16,8},{24,16},{1,25},{9,1},{17,9},{25,17},{2,26},{10... | collective-permute-start | bytes 786440 | tf_op jit(solution)/shard_map/ppermute | solution.py:528
  32.4 5.6 %collective-permute-done.14.rest_3_ = bf16[4,128,256]{2,1,0:T(8,128)(2,1)S(1)} collective-permute-done((bf16[4,128,256]{2,1,0:T(8,128)(2,1)S(1)}, bf16[4,128,256]{2,1,0:T(8,128)(2,1)S(1)}, u32[]{:S(2)}, u32[]{:S(2)}) %collective-permute-start.14) | collective-permute-done | bytes 262176 | tf_op jit(solution)/shard_map/ppermute | solution.py:527
  38.0 0.0 collective-permute-start.15
  38.0 0.3 left.3.rest_0_
  38.3 3.9 %collective-permute-start.6 = (bf16[4,128,256]{2,1,0:T(8,128)(2,1)S(1)}, bf16[4,128,256]{2,1,0:T(8,128)(2,1)S(1)}, u32[]{:S(2)}, u32[]{:S(2)}) collective-permute-start(bf16[4,128,256]{2,1,0:T(8,128)(2,1)S(1)} %bands.2.right_ref.rest_2_), channel_id=1, source_target_pairs={{0,24},{8,0},{16,8},{24,16},{1,25},{9,1},{17,9},{25,17},{2,26},{10... | collective-permute-start | bytes 786440 | tf_op jit(solution)/shard_map/ppermute | solution.py:528
  42.2 3.6 %correlate.6.rest_4_ = f32[4,8,2,256,1024]{4,3,2,1,0:T(8,128)} custom-call(s32[1]{0:T(128)} %bitcast.me_ref, bf16[2,4,256,128]{3,2,1,0:T(8,128)(2,1)S(1)} %left.3.rest_0_, bf16[4,128,256]{2,1,0:T(8,128)(2,1)S(1)} %bands.3.right_ref.rest_1_), custom_call_target="tpu_custom_call" | custom-call | flops 536870912 | bytes 8388608 | tf_op jit(solution)/shard_map/correlate/pallas_call | solution.py:471
  45.8 0.3 left.2.rest_1_.rest_0_
  46.1 0.0 collective-permute-done.4.rest_3_
  46.2 1.2 %collective-permute-start.5 = (bf16[4,128,256]{2,1,0:T(8,128)(2,1)}, bf16[4,128,256]{2,1,0:T(8,128)(2,1)}, u32[]{:S(2)}, u32[]{:S(2)}) collective-permute-start(bf16[4,128,256]{2,1,0:T(8,128)(2,1)} %collective-permute-done.4.rest_3_), channel_id=1, source_target_pairs={{0,8},{8,16},{16,24},{24,0},{1,9},{9,17},{17,25},{25,1},{2,10},{10... | collective-permute-start | bytes 786440 | tf_op jit(solution)/shard_map/ppermute | solution.py:529
  47.3 6.1 %correlate.7.rest_4_ = f32[4,8,2,256,1024]{4,3,2,1,0:T(8,128)} custom-call(s32[1]{0:T(128)} %bitcast.me_ref, bf16[2,4,256,128]{3,2,1,0:T(8,128)(2,1)S(1)} %left.3.rest_0_, bf16[2,4,256,128]{3,2,1,0:T(8,128)(2,1)S(1)} %left.2.rest_1_.rest_0_, bf16[4,128,256]{2,1,0:T(8,128)(2,1)S(1)} %bands.2.right_ref.rest_2_, ...), custom_call_target="tpu_custom_call", output_to_operand_aliasing={{}: (5, {})} | custom-call | flops 1073741824 | bytes 16777216 | tf_op jit(solution)/shard_map/correlate/pallas_call | solution.py:471
  53.5 0.0 collective-permute-done.16.rest_2_
  53.5 7.1 %correlate.8.rest_2_ = f32[4,8,2,256,1024]{4,3,2,1,0:T(8,128)} custom-call(s32[1]{0:T(128)} %bitcast.me_ref, bf16[2,4,256,128]{3,2,1,0:T(8,128)(2,1)S(1)} %left.3.rest_0_, bf16[2,4,256,128]{3,2,1,0:T(8,128)(2,1)S(1)} %left.2.rest_1_.rest_0_, bf16[4,128,256]{2,1,0:T(8,128)(2,1)S(1)} %collective-permute-done.16.rest_2_, ...), custom_call_target="tpu_custom_call", output_to_operand_aliasing={{}: (5, {})} | custom-call | flops 1073741824 | bytes 16777216 | tf_op jit(solution)/shard_map/correlate/pallas_call | solution.py:471
  60.6 0.0 collective-permute-done.15.rest_1_
  60.6 3.6 %correlate.9.rest_2_ = f32[4,8,2,256,1024]{4,3,2,1,0:T(8,128)} custom-call(s32[1]{0:T(128)} %bitcast.me_ref, bf16[2,4,256,128]{3,2,1,0:T(8,128)(2,1)S(1)} %left.3.rest_0_, bf16[4,128,256]{2,1,0:T(8,128)(2,1)S(1)} %collective-permute-done.15.rest_1_, f32[4,8,2,256,1024]{4,3,2,1,0:T(8,128)} %correlate.8.rest_2_), custom_call_target="tpu_custom_call", output_to_operand_aliasing={{}: (3, {})} | custom-call | flops 536870912 | bytes 8388608 | tf_op jit(solution)/shard_map/correlate/pallas_call | solution.py:471
  64.2 0.0 collective-permute-done.6.rest_1_
  64.2 3.6 %correlate.10.rest_2_ = f32[4,8,2,256,1024]{4,3,2,1,0:T(8,128)} custom-call(s32[1]{0:T(128)} %bitcast.me_ref, bf16[2,4,256,128]{3,2,1,0:T(8,128)(2,1)S(1)} %left.2.rest_1_.rest_0_, bf16[4,128,256]{2,1,0:T(8,128)(2,1)S(1)} %collective-permute-done.6.rest_1_, f32[4,8,2,256,1024]{4,3,2,1,0:T(8,128)} %correlate.9.rest_2_), custom_call_target="tpu_custom_call", output_to_operand_aliasing={{}: (3, {})} | custom-call | flops 536870912 | bytes 8388608 | tf_op jit(solution)/shard_map/correlate/pallas_call | solution.py:471
  67.9 0.0 collective-permute-done.5.rest_1_
  67.9 4.6 %correlate.11 = f32[4,8,2,256,1024]{4,3,2,1,0:T(8,128)} custom-call(s32[1]{0:T(128)} %bitcast.me_ref, bf16[2,4,256,128]{3,2,1,0:T(8,128)(2,1)S(1)} %left.2.rest_1_.rest_0_, bf16[4,128,256]{2,1,0:T(8,128)(2,1)} %collective-permute-done.5.rest_1_, f32[4,8,2,256,1024]{4,3,2,1,0:T(8,128)} %correlate.10.rest_2_), custom_call_target="tpu_custom_call", output_to_operand_aliasing={{}: (3, {})} | custom-call | flops 536870912 | bytes 8388608 | tf_op jit(solution)/shard_map/correlate/pallas_call | solution.py:471
  (1 shorter events, 0.0 us)
Async XLA Ops:
  7.4 5.9 %collective-permute-start = (bf16[4,8,16,256]{3,2,1,0:T(8,128)(2,1)S(1)}, bf16[4,8,16,256]{3,2,1,0:T(8,128)(2,1)S(1)}, u32[]{:S(2)}, u32[]{:S(2)}) collective-permute-start(bf16[4,8,16,256]{3,2,1,0:T(8,128)(2,1)S(1)} %get-tuple-element.24), channel_id=1, source_target_pairs={{0,1},{1,0},{2,3},{3,2},{4,5},{5,4},{6,7},{7,6},{8,9},{9,8},{10,11... | collective-permute-start | bytes 786440 | tf_op jit(solution)/shard_map/ppermute | solution.py:508
  8.0 5.6 %collective-permute-start.10 = (bf16[8,16,256]{2,1,0:T(8,128)(2,1)S(1)}, bf16[8,16,256]{2,1,0:T(8,128)(2,1)S(1)}, u32[]{:S(2)}, u32[]{:S(2)}) collective-permute-start(bf16[8,16,256]{2,1,0:T(8,128)(2,1)S(1)} %get-tuple-element.35), channel_id=1, source_target_pairs={{0,4},{1,5},{2,6},{3,7},{4,0},{5,1},{6,2},{7,3},{8,12},{9,13},{10,... | collective-permute-start | bytes 196616 | tf_op jit(solution)/shard_map/ppermute | solution.py:515
  10.6 5.5 %collective-permute-start.11 = (bf16[8,16,256]{2,1,0:T(8,128)(2,1)S(1)}, bf16[8,16,256]{2,1,0:T(8,128)(2,1)S(1)}, u32[]{:S(2)}, u32[]{:S(2)}) collective-permute-start(bf16[8,16,256]{2,1,0:T(8,128)(2,1)S(1)} %get-tuple-element.36), channel_id=1, source_target_pairs={{0,5},{1,4},{2,7},{3,6},{4,1},{5,0},{6,3},{7,2},{8,13},{9,12},{10,... | collective-permute-start | bytes 196616 | tf_op jit(solution)/shard_map/ppermute | solution.py:515
  10.6 6.4 %collective-permute-start.12 = (bf16[8,16,256]{2,1,0:T(8,128)(2,1)S(1)}, bf16[8,16,256]{2,1,0:T(8,128)(2,1)S(1)}, u32[]{:S(2)}, u32[]{:S(2)}) collective-permute-start(bf16[8,16,256]{2,1,0:T(8,128)(2,1)S(1)} %get-tuple-element.37), channel_id=1, source_target_pairs={{0,6},{1,7},{2,4},{3,5},{4,2},{5,3},{6,0},{7,1},{8,14},{9,15},{10,... | collective-permute-start | bytes 196616 | tf_op jit(solution)/shard_map/ppermute | solution.py:515
  13.3 6.0 %collective-permute-start.13 = (bf16[8,16,256]{2,1,0:T(8,128)(2,1)S(1)}, bf16[8,16,256]{2,1,0:T(8,128)(2,1)S(1)}, u32[]{:S(2)}, u32[]{:S(2)}) collective-permute-start(bf16[8,16,256]{2,1,0:T(8,128)(2,1)S(1)} %get-tuple-element.38), channel_id=1, source_target_pairs={{0,7},{1,6},{2,5},{3,4},{4,3},{5,2},{6,1},{7,0},{8,15},{9,14},{10,... | collective-permute-start | bytes 196616 | tf_op jit(solution)/shard_map/ppermute | solution.py:515
  13.3 6.2 %collective-permute-start.7 = (bf16[8,16,256]{2,1,0:T(8,128)(2,1)S(1)}, bf16[8,16,256]{2,1,0:T(8,128)(2,1)S(1)}, u32[]{:S(2)}, u32[]{:S(2)}) collective-permute-start(bf16[8,16,256]{2,1,0:T(8,128)(2,1)S(1)} %get-tuple-element.32), channel_id=1, source_target_pairs={{0,1},{1,0},{2,3},{3,2},{4,5},{5,4},{6,7},{7,6},{8,9},{9,8},{10,11... | collective-permute-start | bytes 196616 | tf_op jit(solution)/shard_map/ppermute | solution.py:515
  13.7 14.6 %collective-permute-start.1 = (bf16[2,8,16,256]{3,2,1,0:T(8,128)(2,1)S(1)}, bf16[2,8,16,256]{3,2,1,0:T(8,128)(2,1)S(1)}, u32[]{:S(2)}, u32[]{:S(2)}) collective-permute-start(bf16[2,8,16,256]{3,2,1,0:T(8,128)(2,1)S(1)} %get-tuple-element.28), channel_id=1, source_target_pairs={{0,2},{1,3},{2,0},{3,1},{4,6},{5,7},{6,4},{7,5},{8,10},{9,11},{10,... | collective-permute-start | bytes 393224 | tf_op jit(solution)/shard_map/ppermute | solution.py:515
  16.0 12.2 %collective-permute-start.2 = (bf16[2,8,16,256]{3,2,1,0:T(8,128)(2,1)S(1)}, bf16[2,8,16,256]{3,2,1,0:T(8,128)(2,1)S(1)}, u32[]{:S(2)}, u32[]{:S(2)}) collective-permute-start(bf16[2,8,16,256]{3,2,1,0:T(8,128)(2,1)S(1)} %get-tuple-element.29), channel_id=1, source_target_pairs={{0,4},{1,5},{2,6},{3,7},{4,0},{5,1},{6,2},{7,3},{8,12},{9,13},{10,... | collective-permute-start | bytes 393224 | tf_op jit(solution)/shard_map/ppermute | solution.py:515
  17.0 11.2 %collective-permute-start.3 = (bf16[2,8,16,256]{3,2,1,0:T(8,128)(2,1)S(1)}, bf16[2,8,16,256]{3,2,1,0:T(8,128)(2,1)S(1)}, u32[]{:S(2)}, u32[]{:S(2)}) collective-permute-start(bf16[2,8,16,256]{3,2,1,0:T(8,128)(2,1)S(1)} %get-tuple-element.30), channel_id=1, source_target_pairs={{0,6},{1,7},{2,4},{3,5},{4,2},{5,3},{6,0},{7,1},{8,14},{9,15},{10,... | collective-permute-start | bytes 393224 | tf_op jit(solution)/shard_map/ppermute | solution.py:515
  19.2 6.1 %collective-permute-start.8 = (bf16[8,16,256]{2,1,0:T(8,128)(2,1)S(1)}, bf16[8,16,256]{2,1,0:T(8,128)(2,1)S(1)}, u32[]{:S(2)}, u32[]{:S(2)}) collective-permute-start(bf16[8,16,256]{2,1,0:T(8,128)(2,1)S(1)} %get-tuple-element.33), channel_id=1, source_target_pairs={{0,2},{1,3},{2,0},{3,1},{4,6},{5,7},{6,4},{7,5},{8,10},{9,11},{10,... | collective-permute-start | bytes 196616 | tf_op jit(solution)/shard_map/ppermute | solution.py:515
  19.5 7.1 %collective-permute-start.9 = (bf16[8,16,256]{2,1,0:T(8,128)(2,1)S(1)}, bf16[8,16,256]{2,1,0:T(8,128)(2,1)S(1)}, u32[]{:S(2)}, u32[]{:S(2)}) collective-permute-start(bf16[8,16,256]{2,1,0:T(8,128)(2,1)S(1)} %get-tuple-element.34), channel_id=1, source_target_pairs={{0,3},{1,2},{2,1},{3,0},{4,7},{5,6},{6,5},{7,4},{8,11},{9,10},{10,... | collective-permute-start | bytes 196616 | tf_op jit(solution)/shard_map/ppermute | solution.py:515
  26.8 11.1 %collective-permute-start.14 = (bf16[4,128,256]{2,1,0:T(8,128)(2,1)S(1)}, bf16[4,128,256]{2,1,0:T(8,128)(2,1)S(1)}, u32[]{:S(2)}, u32[]{:S(2)}) collective-permute-start(bf16[4,128,256]{2,1,0:T(8,128)(2,1)S(1)} %bands.3.right_ref.rest_1_), channel_id=1, source_target_pairs={{0,8},{8,16},{16,24},{24,0},{1,9},{9,17},{17,25},{25,1},{2,10},{10... | collective-permute-start | bytes 786440 | tf_op jit(solution)/shard_map/ppermute | solution.py:527
  28.5 17.6 %collective-permute-start.4 = (bf16[4,128,256]{2,1,0:T(8,128)(2,1)S(1)}, bf16[4,128,256]{2,1,0:T(8,128)(2,1)}, u32[]{:S(2)}, u32[]{:S(2)}) collective-permute-start(bf16[4,128,256]{2,1,0:T(8,128)(2,1)S(1)} %bands.2.right_ref.rest_2_), channel_id=1, source_target_pairs={{0,8},{8,16},{16,24},{24,0},{1,9},{9,17},{17,25},{25,1},{2,10},{10... | collective-permute-start | bytes 786440 | tf_op jit(solution)/shard_map/ppermute | solution.py:527
  30.1 23.3 %collective-permute-start.16 = (bf16[4,128,256]{2,1,0:T(8,128)(2,1)S(1)}, bf16[4,128,256]{2,1,0:T(8,128)(2,1)S(1)}, u32[]{:S(2)}, u32[]{:S(2)}) collective-permute-start(bf16[4,128,256]{2,1,0:T(8,128)(2,1)S(1)} %bands.3.right_ref.rest_1_), channel_id=1, source_target_pairs={{0,24},{8,0},{16,8},{24,16},{1,25},{9,1},{17,9},{25,17},{2,26},{10... | collective-permute-start | bytes 786440 | tf_op jit(solution)/shard_map/ppermute | solution.py:528
  38.0 22.6 %collective-permute-start.15 = (bf16[4,128,256]{2,1,0:T(8,128)(2,1)S(1)}, bf16[4,128,256]{2,1,0:T(8,128)(2,1)S(1)}, u32[]{:S(2)}, u32[]{:S(2)}) collective-permute-start(bf16[4,128,256]{2,1,0:T(8,128)(2,1)S(1)} %collective-permute-done.14.rest_3_), channel_id=1, source_target_pairs={{0,8},{8,16},{16,24},{24,0},{1,9},{9,17},{17,25},{25,1},{2,10},{10... | collective-permute-start | bytes 786440 | tf_op jit(solution)/shard_map/ppermute | solution.py:529
  38.3 25.9 %collective-permute-start.6 = (bf16[4,128,256]{2,1,0:T(8,128)(2,1)S(1)}, bf16[4,128,256]{2,1,0:T(8,128)(2,1)S(1)}, u32[]{:S(2)}, u32[]{:S(2)}) collective-permute-start(bf16[4,128,256]{2,1,0:T(8,128)(2,1)S(1)} %bands.2.right_ref.rest_2_), channel_id=1, source_target_pairs={{0,24},{8,0},{16,8},{24,16},{1,25},{9,1},{17,9},{25,17},{2,26},{10... | collective-permute-start | bytes 786440 | tf_op jit(solution)/shard_map/ppermute | solution.py:528
  46.2 21.7 %collective-permute-start.5 = (bf16[4,128,256]{2,1,0:T(8,128)(2,1)}, bf16[4,128,256]{2,1,0:T(8,128)(2,1)}, u32[]{:S(2)}, u32[]{:S(2)}) collective-permute-start(bf16[4,128,256]{2,1,0:T(8,128)(2,1)} %collective-permute-done.4.rest_3_), channel_id=1, source_target_pairs={{0,8},{8,16},{16,24},{24,0},{1,9},{9,17},{17,25},{25,1},{2,10},{10... | collective-permute-start | bytes 786440 | tf_op jit(solution)/shard_map/ppermute | solution.py:529
